TPU v7x, 256 devices: a whole 4x4x8 slice. The times are simulated.
256 devices in a mesh: orb: 64 (over x, z, core), grp: 4 (over y).
Axes of the slice: x: 4, y: 4, z: 8, core: 2. Of those that a mesh axis runs over, the one named last changes fastest.
Arguments:
- orbitals: float32 [512, 48, 2304], P(('orb', 'grp')), may hold values from -6 to 6
- kernel: float32 [48, 2304], replicated, may hold values from 0.1 to 2
- anchors: int32 [64, 3], replicated, may hold values from 0 to 16
- pair_count: int32 [64], P('orb'), may hold values from 1 to 8, 256 in all
- pair_first: int32 [512], P('orb'), may hold values from 0 to 7
- pair_second: int32 [512], P('orb'), may hold values from 0 to 7
- pair_reach: int32 [512], P('orb'), may hold values from 0 to 2
Outputs:
- gradient: float32 [512, 48, 2304], P('orb', 'grp')
- lagrange: float32 [64, 8, 8], P('orb')
Inputs may be any that keep to these rules, and one draw needn't show every extreme that they name: The live slots of a fragment are its first pair_count slots; some fragment has all 8 live.
All inputs are finite; a program needn't handle non-finite values. No bound on the sum of `pair_count` on one device may be relied on, other than what follows from the above.
Results may differ from a plain program's by a relative error of at most 0.0003.
Values sent between devices are 32-bit elements; how exact they have to be, the bound alone decides.
A program may use at most 128 MiB of HBM per device.

v0:
```python
import math

import jax
import jax.numpy as jnp
from jax import lax
from jax.sharding import PartitionSpec as P

REACH = 2


def passed_along(block, axis, distance):
    devices = range(lax.axis_size(axis))
    route = [((i - distance) % len(devices), i) for i in devices]
    return lax.ppermute(block, axis, route)


def rotate(volume):
    box_edge = volume.shape[0]
    return (
        volume.reshape(box_edge, box_edge, box_edge)
        .transpose(1, 2, 0)
        .reshape(box_edge, box_edge * box_edge)
    )


def matmul(matrix, volume):
    return jnp.dot(
        matrix, volume, precision=lax.Precision.HIGHEST, preferred_element_type=jnp.float32
    )


def displace(volume, delta, sign):
    box_edge = volume.shape[0]
    cube = volume.reshape(box_edge, box_edge, box_edge)
    places = jnp.arange(box_edge, dtype=jnp.int32)
    for axis_index in range(3):
        amount = sign * delta[axis_index]
        cube = jnp.roll(cube, amount, axis=axis_index)
        source = places - amount
        inside = ((source >= 0) & (source < box_edge)).astype(jnp.float32)
        shape = [1, 1, 1]
        shape[axis_index] = box_edge
        cube = cube * inside.reshape(shape)
    return cube.reshape(box_edge, box_edge * box_edge)


def poisson(density, kernel, cosine, sine):
    real_part = rotate(matmul(cosine, density))
    imag_part = rotate(-matmul(sine, density))
    for repeat in range(2):
        new_real = matmul(cosine, real_part) + matmul(sine, imag_part)
        new_imag = matmul(cosine, imag_part) - matmul(sine, real_part)
        real_part, imag_part = (rotate(new_real), rotate(new_imag))
    real_part = real_part * kernel
    imag_part = imag_part * kernel
    for repeat in range(2):
        new_real = matmul(cosine, real_part) - matmul(sine, imag_part)
        new_imag = matmul(cosine, imag_part) + matmul(sine, real_part)
        real_part, imag_part = (rotate(new_real), rotate(new_imag))
    result = rotate(matmul(cosine, real_part) - matmul(sine, imag_part))
    box_edge = density.shape[0]
    return result / float(box_edge**3)


def shards(orbitals, kernel, anchors, pair_count, pair_first, pair_second, pair_reach):
    groups = lax.axis_size("grp")
    fragments = lax.axis_size("orb")
    fragment = lax.axis_index("orb")
    member = lax.axis_index("grp")
    box_edge = orbitals.shape[1]
    indices = jnp.arange(box_edge, dtype=jnp.int32)
    angles = (
        2.0
        * math.pi
        / box_edge
        * (indices[:, None] * indices[None, :] % box_edge).astype(jnp.float32)
    )
    cosine = jnp.cos(angles)
    sine = jnp.sin(angles)
    slots = pair_first.shape[0]
    per_member = slots // groups
    count_here = pair_count[0]

    def pair_terms(slot, phi_first, phi_second, reach):
        partner = (fragment + reach) % fragments
        delta = anchors[partner] - anchors[fragment]
        moved = displace(phi_second, delta, 1)
        potential = poisson(phi_first * moved, kernel, cosine, sine)
        weight = (slot < count_here).astype(jnp.float32)
        back = displace(potential * phi_first, delta, -1)
        return (weight * potential * moved, weight * back)

    own_orbitals = lax.all_gather(orbitals, "grp", axis=0, tiled=True)
    neighbours = [own_orbitals]
    for reach_index in range(1, REACH + 1):
        neighbours.append(passed_along(own_orbitals, "orb", -reach_index))
    nearby = jnp.stack(neighbours)
    own_fragment = nearby[0]

    def solve_slot(turn, accum):
        slot = member + groups * turn
        first = pair_first[slot]
        second = pair_second[slot]
        reach = pair_reach[slot]
        forward, back = pair_terms(slot, nearby[0, first], nearby[reach, second], reach)
        accum = accum.at[0, first].add(forward)
        accum = accum.at[reach, second].add(back)
        return accum

    empty = jnp.zeros(nearby.shape, jnp.float32)
    accum = lax.fori_loop(0, per_member, solve_slot, empty)
    total = accum[0]
    for reach_index in range(1, REACH + 1):
        total = total + passed_along(accum[reach_index], "orb", reach_index)
    action = lax.psum_scatter(total, "grp", scatter_dimension=1, tiled=True)
    slab_rows = box_edge // groups
    phi_slab = lax.dynamic_slice_in_dim(own_fragment, member * slab_rows, slab_rows, 1)
    frag_size = phi_slab.shape[0]
    phi_flat = phi_slab.reshape(frag_size, -1)
    action_flat = action.reshape(frag_size, -1)
    partial_correlation = jnp.dot(
        phi_flat, action_flat.T, precision=lax.Precision.HIGHEST, preferred_element_type=jnp.float32
    ) / float(box_edge**3)
    correlation = lax.psum(partial_correlation, "grp")
    lagrange = 0.5 * (correlation + correlation.T)
    projected = jnp.dot(
        lagrange.T, phi_flat, precision=lax.Precision.HIGHEST, preferred_element_type=jnp.float32
    )
    gradient = action - projected.reshape(action.shape)
    return (gradient, lagrange[None])


def solution(mesh):
    placed = (P(("orb", "grp"), None, None), P(), P(), P("orb"), P("orb"), P("orb"), P("orb"))
    return jax.shard_map(
        shards,
        mesh=mesh,
        in_specs=placed,
        out_specs=(P("orb", "grp", None), P("orb", None, None)),
        check_vma=False,
    )
```

profile of v0, /device:TPU:1, one launch (start us, length us, event | category | flops | bytes accessed | tf_op | source)
XLA Modules:
  0.0 652.7 jit_solution(1310700272529633124)
XLA Ops:
  7.9 50.8 %all-gather.2.cloned.1.call-done = f32[8,48,2304]{2,1,0:T(8,128)} async-done(((f32[2,48,2304]{2,1,0:T(8,128)}), f32[8,48,2304]{2,1,0:T(8,128)}) %all-gather.2.cloned.1.call-update) | async-done | bytes 3538960 | tf_op jit(solution)/shard_map/all_gather | solution.py:93
  58.8 5.2 collective-permute-start.1
  65.8 73.5 %collective-permute-done.1 = f32[8,48,2304]{2,1,0:T(8,128)} collective-permute-done((f32[8,48,2304]{2,1,0:T(8,128)}, f32[8,48,2304]{2,1,0:T(8,128)}, u32[]{:S(2)}, u32[]{:S(2)}) %collective-permute-start.1) | collective-permute-done | bytes 3538976 | tf_op jit(solution)/shard_map/ppermute | solution.py:14
  139.3 36.0 %collective-permute-done = f32[8,48,2304]{2,1,0:T(8,128)} collective-permute-done((f32[8,48,2304]{2,1,0:T(8,128)}, f32[8,48,2304]{2,1,0:T(8,128)}, u32[]{:S(2)}, u32[]{:S(2)}) %collective-permute-start) | collective-permute-done | bytes 3538976 | tf_op jit(solution)/shard_map/ppermute | solution.py:14
  175.3 8.9 %pad_maximum_fusion = f32[3,8,48,2304]{3,2,1,0:T(8,128)} fusion(f32[1,8,48,2304]{3,2,1,0:T(8,128)} %bitcast.2, f32[1,8,48,2304]{3,2,1,0:T(8,128)} %bitcast.1, f32[1,8,48,2304]{3,2,1,0:T(8,128)} %bitcast.235), kind=kLoop, calls=%fused_computation.188 | loop fusion | flops 5308416 | bytes 21233664 | tf_op jit(solution)/shard_map/stack | solution.py:97
  184.2 5.1 broadcast_in_dim.33
  189.3 270.4 %while.19 = (s32[]{:T(128)}, f32[3,8,48,2304]{3,2,1,0:T(8,128)}, s32[]{:T(128)}, s32[8]{0:T(128)S(1)}, f32[3,8,48,2304]{3,2,1,0:T(8,128)}, /*index=5*/s32[8]{0:T...) while((s32[]{:T(128)}, f32[3,8,48,2304]{3,2,1,0:T(8,128)}, ...), condition=%wide.region_3.7_spmd.clone.clone, body=%wide.region_0.6_spmd.clone.clone.sunk | while | flops 1278749184 | bytes 73439736 | solution.py:111
  259.5 2.6 fusion.336
  264.2 2.8 reshape.573
  267.0 2.7 copy.92
  272.9 2.8 reshape.575
  275.7 2.7 copy.93
  316.6 3.0 fusion.345
  385.6 2.8 reshape.573
  388.4 2.7 copy.92
  394.3 2.8 reshape.575
  397.1 2.7 copy.93
  438.0 3.0 fusion.345
  459.8 10.2 %copy.51 = f32[3,8,48,2304]{3,1,2,0:T(8,128)S(1)} copy(f32[3,8,48,2304]{3,2,1,0:T(8,128)} %get-tuple-element.422) | data formatting | bytes 21233664 | tf_op jit(solution)/shard_map/while | solution.py:111
  471.8 71.1 %collective-permute-done.2 = f32[8,48,2304]{2,0,1:T(8,128)S(1)} collective-permute-done((f32[8,48,2304]{2,0,1:T(8,128)S(1)}, f32[8,48,2304]{2,0,1:T(8,128)S(1)}, u32[]{:S(2)}, u32[]{:S(2)}) %collective-permute-start.2) | collective-permute-done | bytes 3538976 | tf_op jit(solution)/shard_map/ppermute | solution.py:14
  542.9 50.8 %collective-permute-done.3 = f32[8,48,2304]{2,0,1:T(8,128)S(1)} collective-permute-done((f32[8,48,2304]{2,0,1:T(8,128)S(1)}, f32[8,48,2304]{2,0,1:T(8,128)S(1)}, u32[]{:S(2)}, u32[]{:S(2)}) %collective-permute-start.3) | collective-permute-done | bytes 3538976 | tf_op jit(solution)/shard_map/ppermute | solution.py:14
  597.8 35.1 %reduce-scatter.2.cloned.1.call-done = f32[8,12,2304]{2,0,1:T(8,128)} async-done(((f32[8,48,2304]{2,0,1:T(8,128)}), f32[8,12,2304]{2,0,1:T(8,128)}) %reduce-scatter.2.cloned.1.call-update) | async-done | bytes 884752 | tf_op jit(solution)/shard_map/reduce_scatter | solution.py:115
  632.9 3.4 fusion.189
  636.3 6.5 %psum.7 = f32[8,8]{1,0:T(8,128)S(1)} all-reduce(f32[8,8]{1,0:T(8,128)S(1)} %fusion.189), channel_id=1, replica_groups=mesh['orb'=64,'grp'=4] {'grp'}, use_global_device_ids=true, to_apply=%region_5.9 | all-reduce | flops 64 | bytes 512 | tf_op jit(solution)/shard_map/psum | solution.py:124
  (179 shorter events, 201.1 us)
Async XLA Ops:
  7.2 51.6 %all-gather.2.cloned.1.call-start = ((), (), s32[]{:S(2)}) async-start(), calls=%async_computation.1 | async-start | bytes 4423680 | tf_op jit(solution)/shard_map/all_gather | solution.py:93
  7.9 625.0 %reduce-scatter.2.cloned.1.call-start = ((), (), s32[]{:S(2)}) async-start(), calls=%async_computation.2 | async-start | bytes 4423680 | tf_op jit(solution)/shard_map/reduce_scatter | solution.py:115
  58.8 80.5 %collective-permute-start.1 = (f32[8,48,2304]{2,1,0:T(8,128)}, f32[8,48,2304]{2,1,0:T(8,128)}, u32[]{:S(2)}, u32[]{:S(2)}) collective-permute-start(f32[8,48,2304]{2,1,0:T(8,128)} %all-gather.2.cloned.1.call-done), channel_id=1, source_target_pairs={{8,0},{12,4},{16,8},{20,12},{24,16},{28,20},{32,24},{36,28},{40,32... | collective-permute-start | bytes 10616840 | tf_op jit(solution)/shard_map/ppermute | solution.py:14
  63.9 111.3 %collective-permute-start = (f32[8,48,2304]{2,1,0:T(8,128)}, f32[8,48,2304]{2,1,0:T(8,128)}, u32[]{:S(2)}, u32[]{:S(2)}) collective-permute-start(f32[8,48,2304]{2,1,0:T(8,128)} %all-gather.2.cloned.1.call-done), channel_id=1, source_target_pairs={{4,0},{8,4},{12,8},{16,12},{20,16},{24,20},{28,24},{32,28},{36,32}... | collective-permute-start | bytes 10616840 | tf_op jit(solution)/shard_map/ppermute | solution.py:14
  184.2 5.1 copy-start
  184.2 5.1 copy-start.8
  184.2 5.1 copy-start.9
  184.2 5.1 copy-start.10
  184.2 5.1 copy-start.11
  184.2 5.1 copy-start.12
  229.0 2.5 copy-start.5
  244.3 2.6 copy-start.2
  259.5 2.6 copy-start.3
  281.0 2.6 copy-start.1
  296.2 2.6 copy-start.4
  309.0 2.5 copy-start.6
  365.7 2.6 copy-start.2
  380.9 2.6 copy-start.3
  402.4 2.6 copy-start.1
  417.7 2.6 copy-start.4
  430.4 2.5 copy-start.6
  470.4 72.6 %collective-permute-start.2 = (f32[8,48,2304]{2,0,1:T(8,128)S(1)}, f32[8,48,2304]{2,0,1:T(8,128)S(1)}, u32[]{:S(2)}, u32[]{:S(2)}) collective-permute-start(f32[8,48,2304]{2,0,1:T(8,128)S(1)} %get-tuple-element.564), channel_id=1, source_target_pairs={{252,0},{0,4},{4,8},{8,12},{12,16},{16,20},{20,24},{24,28},{28,32}... | collective-permute-start | bytes 10616840 | tf_op jit(solution)/shard_map/ppermute | solution.py:14
  470.5 123.3 %collective-permute-start.3 = (f32[8,48,2304]{2,0,1:T(8,128)S(1)}, f32[8,48,2304]{2,0,1:T(8,128)S(1)}, u32[]{:S(2)}, u32[]{:S(2)}) collective-permute-start(f32[8,48,2304]{2,0,1:T(8,128)S(1)} %get-tuple-element.565), channel_id=1, source_target_pairs={{248,0},{252,4},{0,8},{4,12},{8,16},{12,20},{16,24},{20,28},{24,32... | collective-permute-start | bytes 10616840 | tf_op jit(solution)/shard_map/ppermute | solution.py:14
  632.9 10.6 %copy-start.7 = (f32[8,12,2304]{2,0,1:T(8,128)S(1)}, f32[8,12,2304]{2,0,1:T(8,128)}, u32[]{:S(2)}) copy-start(f32[8,12,2304]{2,0,1:T(8,128)} %reduce-scatter.2.cloned.1.call-done) | copy-start | bytes 2654212
  (1 other events, 2.5 us)
Sparse Core Ops, SparseCore 0:
  9.8 48.9 all-gather.1
  596.3 36.5 reduce-scatter.1
where the time goes:
time: 660 us; the launch traced here: 653 us
  waiting for transfers between devices  318 us (48%)
  local copies, waits for them, and re-layouts  147 us (22%)
  matrix products  69.6 us (11%)
  loops' own time  49.9 us (8%)
  other arithmetic  39.3 us (6%)
  between operations  14.3 us (2%)
  starting transfers between devices  7.76 us (1%)
    ppermute x4, waiting for transfers between devices, passed_along(): return lax.ppermute(block, axis, route)  231 us
    dot_general x40, matrix products, matmul(): jnp.dot(matrix, volume, precision=lax.Precision.HIGHEST, preferred_elemen...  64 us
    reshape x20, local copies, waits for them, and re-layouts, rotate(): volume.reshape(box_edge, box_edge, box_edge).transpose(1, 2, 0)  51.2 us
    all_gather x1, waiting for transfers between devices, shards(): own_orbitals = lax.all_gather(orbitals, 'grp', axis=0, tiled=True)  50.8 us
    another operation x1, loops' own time, shards(): accum = lax.fori_loop(0, per_member, solve_slot, empty)  49.9 us
    reshape x20, local copies, waits for them, and re-layouts, rotate(): return volume.reshape(box_edge, box_edge, box_edge).transpose(1, 2, 0).re...  42.2 us
    reduce_scatter x1, waiting for transfers between devices, shards(): action = lax.psum_scatter(total, 'grp', scatter_dimension=1, tiled=True)  35.1 us
  transfers between devices with their start and end apart: 6, of which 6 were waited for; matrix products, arithmetic and copies ran while one was open for 0% of the time, Pallas kernels for 0%

commit v1 on v0

v1 whole, which is shorter than its diff:
```python
import functools
import math

import jax
import jax.numpy as jnp
import ml_dtypes
import numpy as np
from jax import lax
from jax.experimental import pallas as pl
from jax.experimental.pallas import tpu as pltpu
from jax.sharding import PartitionSpec as P

MESH = pl.DeviceIdType.MESH
B = 48
FRAG = 8
GRP = 4
TURNS = 2
TILES = 18
SLAB = 216
ROWS = 864
HALF = 25
CH = 152
PADX = 16
PADT = 8


def split(a):
    a = a.astype(np.float32)
    head = a.astype(ml_dtypes.bfloat16)
    tail = (a - head.astype(np.float32)).astype(ml_dtypes.bfloat16)
    return head, tail


@functools.lru_cache(None)
def tables():
    c, kx = np.meshgrid(np.arange(6), np.arange(HALF), indexing="ij")
    c, kx = c.reshape(-1, 1), kx.reshape(-1, 1)
    a, x = np.meshgrid(np.arange(6), np.arange(B), indexing="ij")
    a, x = a.reshape(1, -1), x.reshape(1, -1)
    theta = 2 * np.pi * ((8 * c * a + kx * x) % 48) / 48
    left = np.zeros((2 * CH, 288))
    left[:150] = np.cos(theta)
    left[CH:CH + 150] = -np.sin(theta)
    head, tail = split(left)
    fwd_left = np.concatenate([head, head, tail], axis=1)
    inv_left = np.concatenate([head.T, head.T, tail.T], axis=1)
    b, z = np.meshgrid(np.arange(8), np.arange(B), indexing="ij")
    b, z = b.reshape(-1), z.reshape(-1)
    phi = 2 * np.pi * ((6 * np.outer(b, b) + np.outer(z, z)) % 48) / 48
    head, tail = split(np.concatenate([np.cos(phi), -np.sin(phi)], axis=1))
    right = np.concatenate([head, head, tail], axis=0)
    turn = 2 * np.pi * ((c * b[None, :]) % 48) / 48
    twiddle = np.zeros((2, CH, 384), np.float32)
    twiddle[0, :150] = np.cos(turn)
    twiddle[1, :150] = -np.sin(turn)
    return fwd_left, inv_left, right, twiddle


def mode_table(kernel):
    cube = kernel.reshape(B, B, B)
    flipped = jnp.roll(jnp.flip(cube, (0, 1, 2)), (1, 1, 1), (0, 1, 2))
    even = (cube[:HALF] + flipped[:HALF]) * 0.5
    weight = np.full((HALF, 1, 1), 2.0 / B**3, np.float32)
    weight[0] = weight[HALF - 1] = 1.0 / B**3
    even = (even * weight).reshape(HALF, 8, 6, B).transpose(2, 0, 1, 3).reshape(6 * HALF, 384)
    return jnp.pad(even, ((0, CH - 6 * HALF), (0, 0)))


def halves(value):
    head = value.astype(jnp.bfloat16)
    return head, (value - head.astype(jnp.float32)).astype(jnp.bfloat16)


def dot(a, b):
    return jnp.dot(a, b, preferred_element_type=jnp.float32)


def shifted(source, offset, emit):
    d0, d1, d2 = offset
    flat = 48 * d1 + d2 + 1024
    tile = lax.shift_right_logical(flat, 7) - 8
    lane_by = lax.bitwise_and(flat, 127)
    lane = lax.broadcasted_iota(jnp.int32, (B, 128), 1)
    late = lane >= lane_by
    insides = []
    for k in range(3):
        z = lax.rem(lane + 128 * k, B) - d2
        insides.append((z >= 0) & (z < B))
    before = None
    for t in range(-1, TILES):
        block = source[t - tile + PADT, pl.ds(PADX - d0, B), :]
        block = pltpu.roll(block, lane_by, 1)
        if t >= 0:
            emit(t, jnp.where(insides[t % 3], jnp.where(late, block, before), 0.0))
        before = block


def pair_kernel(first_ref, second_ref, modes_ref, fwd_left, inv_left, right, twiddle,
                anchors, reach_ref, out_ref, padded, boxes, moved, stack, wide, spec, volume):
    frag, member = lax.axis_index("orb"), lax.axis_index("grp")

    def offset_of(turn):
        partner = lax.rem(frag + reach_ref[member + GRP * turn], lax.axis_size("orb"))
        return [anchors[partner, k] - anchors[frag, k] for k in range(3)]

    padded[...] = jnp.zeros_like(padded)

    def at(t):
        return slice(48 * (t // 3), 48 * (t // 3) + 48), slice(128 * (t % 3), 128 * (t % 3) + 128)

    for turn in range(TURNS):
        for s in range(GRP):
            boxes[0, pl.ds(SLAB * s, SLAB), :] = first_ref[s, turn]
            boxes[1, pl.ds(SLAB * s, SLAB), :] = second_ref[s, turn]
        for t in range(TILES):
            padded[t + PADT, pl.ds(PADX, B), :] = boxes[1, pl.ds(t, B, stride=TILES), :]

        def emit(t, block):
            moved[turn, t] = block
            density = boxes[0, pl.ds(t, B, stride=TILES), :] * block
            head, tail = halves(density)
            rows, lanes = at(t)
            lanes = slice(384 * turn + lanes.start, 384 * turn + lanes.stop)
            stack[rows.start:rows.stop, lanes] = head
            stack[288 + rows.start:288 + rows.stop, lanes] = tail
            stack[576 + rows.start:576 + rows.stop, lanes] = head

        shifted(padded, offset_of(turn), emit)

    volume[0:2 * CH, :] = dot(fwd_left[...], stack[0:864, :])
    tr, ti = twiddle[0], twiddle[1]

    def put(row, value):
        head, tail = halves(value)
        wide[row:row + CH, 0:384] = head
        wide[row:row + CH, 384:768] = tail
        wide[row:row + CH, 768:1152] = head

    for turn in range(TURNS):
        re = volume[0:CH, 384 * turn:384 * turn + 384]
        im = volume[CH:2 * CH, 384 * turn:384 * turn + 384]
        put(2 * CH * turn, re * tr - im * ti)
        put(2 * CH * turn + CH, re * ti + im * tr)
    spec[...] = dot(wide[...], right[...])
    table = modes_ref[...]
    for turn in range(TURNS):
        row = 2 * CH * turn
        re = spec[row:row + CH, 0:384] - spec[row + CH:row + 2 * CH, 384:768]
        im = spec[row:row + CH, 384:768] + spec[row + CH:row + 2 * CH, 0:384]
        put(row, re * table)
        put(row + CH, im * table)
    spec[...] = dot(wide[...], right[...])
    for turn in range(TURNS):
        row = 2 * CH * turn
        re = spec[row:row + CH, 0:384] + spec[row + CH:row + 2 * CH, 384:768]
        im = spec[row + CH:row + 2 * CH, 0:384] - spec[row:row + CH, 384:768]
        lanes = slice(384 * turn, 384 * turn + 384)
        for part, value in enumerate((re * tr + im * ti, im * tr - re * ti)):
            head, tail = halves(value)
            stack[CH * part:CH * part + CH, lanes] = head
            stack[304 + CH * part:304 + CH * part + CH, lanes] = tail
            stack[608 + CH * part:608 + CH * part + CH, lanes] = head
    volume[0:288, :] = dot(inv_left[...], stack[...])

    for turn in range(TURNS):
        for s in range(GRP):
            boxes[0, pl.ds(SLAB * s, SLAB), :] = first_ref[s, turn]
        for t in range(TILES):
            rows, lanes = at(t)
            potential = volume[rows, 384 * turn + lanes.start:384 * turn + lanes.stop]
            out_ref[turn, 0, pl.ds(t, B, stride=TILES), :] = potential * moved[turn, t]
            padded[t + PADT, pl.ds(PADX, B), :] = potential * boxes[0, pl.ds(t, B, stride=TILES), :]

        def emit(t, block):
            out_ref[turn, 1, pl.ds(t, B, stride=TILES), :] = block

        shifted(padded, [-d for d in offset_of(turn)], emit)


def pair_terms(first, second, modes, anchors, reach):
    fwd_left, inv_left, right, twiddle = tables()
    vmem, smem = pl.BlockSpec(memory_space=pltpu.VMEM), pl.BlockSpec(memory_space=pltpu.SMEM)
    return pl.pallas_call(
        pair_kernel,
        out_shape=jax.ShapeDtypeStruct((TURNS, 2, ROWS, 128), jnp.float32),
        in_specs=[vmem] * 7 + [smem] * 2,
        out_specs=vmem,
        scratch_shapes=[
            pltpu.VMEM((TILES + 2 * PADT, B + 2 * PADX, 128), jnp.float32),
            pltpu.VMEM((2, ROWS, 128), jnp.float32),
            pltpu.VMEM((TURNS, TILES, B, 128), jnp.float32),
            pltpu.VMEM((912, 768), jnp.bfloat16),
            pltpu.VMEM((2 * TURNS * CH, 1152), jnp.bfloat16),
            pltpu.VMEM((2 * TURNS * CH, 768), jnp.float32),
            pltpu.VMEM((2 * CH, 768), jnp.float32),
        ],
        compiler_params=pltpu.CompilerParams(vmem_limit_bytes=60 << 20),
        name="pair_terms",
    )(first, second, modes, jnp.asarray(fwd_left), jnp.asarray(inv_left), jnp.asarray(right),
      jnp.asarray(twiddle), anchors, reach)


def gather_kernel(terms_ref, count, first, second, reach, acc_ref):
    acc_ref[...] = jnp.zeros_like(acc_ref)
    for slot in range(GRP * TURNS):
        @pl.when(slot < count[0])
        def _():
            turn, member = slot // GRP, slot % GRP
            acc_ref[0, first[slot]] += terms_ref[turn, 0, member]
            acc_ref[reach[slot], second[slot]] += terms_ref[turn, 1, member]


def gathered(terms, count, first, second, reach):
    vmem, smem = pl.BlockSpec(memory_space=pltpu.VMEM), pl.BlockSpec(memory_space=pltpu.SMEM)
    return pl.pallas_call(
        gather_kernel,
        out_shape=jax.ShapeDtypeStruct((3, FRAG, SLAB, 128), jnp.float32),
        in_specs=[vmem] + [smem] * 4,
        out_specs=vmem,
        compiler_params=pltpu.CompilerParams(vmem_limit_bytes=40 << 20),
        name="gathered",
    )(terms, count, first, second, reach)


def correlate_kernel(phi_ref, own_ref, one_ref, two_ref, action_ref, total_ref, block, landed, send_sem, recv_sem):
    me = lax.axis_index("grp")
    barrier = pltpu.get_barrier_semaphore()
    for step in range(1, GRP):
        pl.semaphore_signal(barrier, inc=1, device_id={"grp": lax.rem(me + step, GRP)}, device_id_type=MESH)
    row = lax.broadcasted_iota(jnp.int32, (FRAG, 128), 0)
    lane = lax.broadcasted_iota(jnp.int32, (FRAG, 128), 1)
    for b in range(FRAG):
        action_ref[b] = own_ref[b] + one_ref[b] + two_ref[b]
    total = jnp.zeros((FRAG, 128), jnp.float32)
    for b in range(FRAG):
        act = action_ref[b]
        for a in range(FRAG):
            part = jnp.sum(phi_ref[a] * act, axis=0, keepdims=True)
            part = jnp.sum(part, axis=1, keepdims=True)
            total = total + jnp.where((row == a) & (lane == b), part, 0.0)
    block[...] = total
    pl.semaphore_wait(barrier, GRP - 1)
    copies = []
    for step in range(1, GRP):
        copies.append(pltpu.make_async_remote_copy(
            src_ref=block, dst_ref=landed.at[step], send_sem=send_sem.at[step], recv_sem=recv_sem.at[step],
            device_id={"grp": lax.rem(me + step, GRP)}, device_id_type=MESH))
    for copy in copies:
        copy.start()
    for copy in copies:
        copy.wait()
    total_ref[...] = ((block[...] + landed[2]) + (landed[1] + landed[3])) / float(B**3)


def correlated(phi, own, one, two):
    vmem = pl.BlockSpec(memory_space=pltpu.VMEM)
    return pl.pallas_call(
        correlate_kernel,
        out_shape=(jax.ShapeDtypeStruct((FRAG, SLAB, 128), jnp.float32),
                   jax.ShapeDtypeStruct((FRAG, 128), jnp.float32)),
        in_specs=[vmem] * 4,
        out_specs=(vmem, vmem),
        scratch_shapes=[
            pltpu.VMEM((FRAG, 128), jnp.float32),
            pltpu.VMEM((GRP, FRAG, 128), jnp.float32),
            pltpu.SemaphoreType.DMA((GRP,)),
            pltpu.SemaphoreType.DMA((GRP,)),
        ],
        compiler_params=pltpu.CompilerParams(
            collective_id=0, has_side_effects=True, vmem_limit_bytes=40 << 20),
        name="correlated",
    )(phi, own, one, two)


def project_kernel(phi_ref, action_ref, total_ref, gradient_ref, lagrange_ref):
    total = total_ref[...][:, 0:FRAG]
    lagrange = 0.5 * (total + total.T)
    lagrange_ref[0] = lagrange
    for a in range(FRAG):
        for t in range(TILES):
            value = action_ref[a, pl.ds(t, 12, stride=TILES), :]
            for b in range(FRAG):
                value = value - lagrange[b:b + 1, a:a + 1] * phi_ref[b, pl.ds(t, 12, stride=TILES), :]
            gradient_ref[a, :, 128 * t:128 * t + 128] = value


def projected(phi, action, total):
    vmem = pl.BlockSpec(memory_space=pltpu.VMEM)
    return pl.pallas_call(
        project_kernel,
        out_shape=(jax.ShapeDtypeStruct((FRAG, 12, B * B), jnp.float32),
                   jax.ShapeDtypeStruct((1, FRAG, FRAG), jnp.float32)),
        in_specs=[vmem] * 3,
        out_specs=(vmem, vmem),
        compiler_params=pltpu.CompilerParams(vmem_limit_bytes=40 << 20),
        name="projected",
    )(phi, action, total)


def passed_along(block, distance):
    count = lax.axis_size("orb")
    return lax.ppermute(block, "orb", [((i - distance) % count, i) for i in range(count)])


def shards(orbitals, kernel, anchors, pair_count, pair_first, pair_second, pair_reach):
    phi = lax.all_to_all(orbitals.reshape(2, GRP, SLAB, 128), "grp", split_axis=1, concat_axis=0, tiled=True)
    phi = phi.reshape(FRAG, SLAB, 128)
    ahead = [passed_along(phi, -r) for r in (1, 2)]
    modes = mode_table(kernel)
    nearby = jnp.stack([phi] + ahead)
    order = np.arange(GRP * TURNS).reshape(TURNS, GRP).T.reshape(-1)
    first = phi[pair_first[order]].reshape(GRP, TURNS, SLAB, 128)
    second = nearby[pair_reach[order], pair_second[order]].reshape(GRP, TURNS, SLAB, 128)
    first = lax.all_to_all(first, "grp", split_axis=0, concat_axis=0, tiled=True)
    second = lax.all_to_all(second, "grp", split_axis=0, concat_axis=0, tiled=True)
    terms = pair_terms(first, second, modes, anchors, pair_reach)
    terms = terms.reshape(TURNS, 2, GRP, SLAB, 128)
    terms = lax.all_to_all(terms, "grp", split_axis=2, concat_axis=2, tiled=True)
    acc = gathered(terms, pair_count, pair_first, pair_second, pair_reach)
    one, two = (passed_along(acc[r], r) for r in (1, 2))
    action, total = correlated(phi, acc[0], one, two)
    return projected(phi, action, total)


def solution(mesh):
    placed = (P(("orb", "grp"), None, None), P(), P(), P("orb"), P("orb"), P("orb"), P("orb"))
    return jax.shard_map(
        shards,
        mesh=mesh,
        in_specs=placed,
        out_specs=(P("orb", "grp", None), P("orb", None, None)),
        check_vma=False,
    )
```

time: 660 us -> 157 us (0.24)
  waiting for transfers between devices: 318 us -> 62.6 us
  local copies, waits for them, and re-layouts: 147 us -> 21.4 us
  matrix products: 69.6 us -> 0 us
  loops' own time: 49.9 us -> 0 us
  other arithmetic: 39.3 us -> 3.95 us
  starting transfers between devices: 7.76 us -> 33.3 us
  Pallas kernels: 0 us -> 16 us
  between operations: 14.3 us -> 1.51 us
  blocking collectives: 6.54 us -> 17.3 us
    ppermute x4, waiting for transfers between devices: 231 us -> 47.2 us  [passed_along(): lax.ppermute(block, 'orb', [((i - distance) % count, i) for i in range(co...]
    reshape x42 -> x5, local copies, waits for them, and re-layouts: 95.9 us -> 5.48 us  [the longest x1 2.82 us: shards(): terms = terms.reshape(TURNS, 2, GRP, SLAB, 128)]
    dot_general x42 -> x0, matrix products: 69.6 us -> none  [the longest x40 64 us: matmul(): jnp.dot(matrix, volume, precision=lax.Precision.HIGHEST, preferred_elemen...]
    all_gather x1 -> x0, waiting for transfers between devices: 50.8 us -> none  [shards(): own_orbitals = lax.all_gather(orbitals, 'grp', axis=0, tiled=True)]
    another operation x1 -> x0, loops' own time: 49.9 us -> none  [shards(): accum = lax.fori_loop(0, per_member, solve_slot, empty)]
    reduce_scatter x1 -> x0, waiting for transfers between devices: 35.1 us -> none  [shards(): action = lax.psum_scatter(total, 'grp', scatter_dimension=1, tiled=True)]
    all_to_all x0 -> x1, blocking collectives: none -> 17.3 us  [shards(): lax.all_to_all(orbitals.reshape(2, GRP, SLAB, 128), 'grp', split_axis=1,...]
    pallas_call x0 -> x4, Pallas kernels: none -> 16 us  [the longest x1 9.48 us: pair_terms(): pl.pallas_call(pair_kernel, out_shape=jax.ShapeDtypeStruct((TURNS, 2, ROW...]
  transfers between devices with their start and end apart: 6 -> 7, of which waited for: 6 -> 5; matrix products, arithmetic and copies ran while one was open for 0% -> 11% of each run, Pallas kernels for 0% -> 0%
where the time goes in v1:
time: 157 us; the launch traced here: 156 us
  waiting for transfers between devices  62.6 us (40%)
  starting transfers between devices  33.3 us (21%)
  local copies, waits for them, and re-layouts  21.4 us (14%)
  blocking collectives  17.3 us (11%)
  Pallas kernels  16 us (10%)
  other arithmetic  3.95 us (3%)
    ppermute x4, waiting for transfers between devices, passed_along(): lax.ppermute(block, 'orb', [((i - distance) % count, i) for i in range(co...  47.2 us
    ppermute x4, starting transfers between devices, passed_along(): lax.ppermute(block, 'orb', [((i - distance) % count, i) for i in range(co...  20.4 us
    all_to_all x1, blocking collectives, shards(): lax.all_to_all(orbitals.reshape(2, GRP, SLAB, 128), 'grp', split_axis=1,...  17.3 us
    all_to_all x1, waiting for transfers between devices, shards(): lax.all_to_all(terms, 'grp', split_axis=2, concat_axis=2, tiled=True)  15.3 us
    pallas_call x1, Pallas kernels, pair_terms(): pl.pallas_call(pair_kernel, out_shape=jax.ShapeDtypeStruct((TURNS, 2, ROW...  9.48 us
    slice x7, local copies, waits for them, and re-layouts, mode_table(): flipped = jnp.roll(jnp.flip(cube, (0, 1, 2)), (1, 1, 1), (0, 1, 2))  4.59 us
    all_to_all x1, starting transfers between devices, shards(): lax.all_to_all(first, 'grp', split_axis=0, concat_axis=0, tiled=True)  4.38 us
    all_to_all x1, starting transfers between devices, shards(): lax.all_to_all(second, 'grp', split_axis=0, concat_axis=0, tiled=True)  4.37 us
  transfers between devices with their start and end apart: 7, of which 5 were waited for; matrix products, arithmetic and copies ran while one was open for 11% of the time, Pallas kernels for 0%

profile of v1, /device:TPU:1, one launch (start us, length us, event | category | flops | bytes accessed | tf_op | source)
XLA Modules:
  0.0 156.0 jit_solution(1244512665019421767)
XLA Ops:
  0.6 1.2 reshape.72
  1.9 17.3 %all_to_all.30 = f32[2,4,216,128]{3,2,0,1:T(8,128)S(1)} all-to-all(f32[2,4,216,128]{3,2,0,1:T(8,128)S(1)} %copy.25), channel_id=1, replica_groups=mesh['orb'=64,'grp'=4] {'grp'}, dimensions={1} | all-to-all | bytes 1769472 | tf_op jit(solution)/shard_map/all_to_all | solution.py:306
  19.2 7.8 %collective-permute-start.1 = (f32[8,216,128]{2,1,0:T(8,128)S(1)}, f32[8,216,128]{2,1,0:T(8,128)S(1)}, u32[]{:S(2)}, u32[]{:S(2)}) collective-permute-start(f32[8,216,128]{2,1,0:T(8,128)S(1)} %bitcast.36), channel_id=1, source_target_pairs={{8,0},{12,4},{16,8},{20,12},{24,16},{28,20},{32,24},{36,28},{40,32... | collective-permute-start | bytes 2654216 | tf_op jit(solution)/shard_map/ppermute | solution.py:302
  27.0 2.1 %collective-permute-start = (f32[8,216,128]{2,1,0:T(8,128)S(1)}, f32[8,216,128]{2,1,0:T(8,128)S(1)}, u32[]{:S(2)}, u32[]{:S(2)}) collective-permute-start(f32[8,216,128]{2,1,0:T(8,128)S(1)} %bitcast.37), channel_id=1, source_target_pairs={{4,0},{8,4},{12,8},{16,12},{20,16},{24,20},{28,24},{32,28},{36,32}... | collective-permute-start | bytes 2654216 | tf_op jit(solution)/shard_map/ppermute | solution.py:302
  29.8 1.5 gather_fusion.1
  31.3 4.4 %all-to-all-start.1 = ((f32[4,2,216,128]{3,2,1,0:T(8,128)}), f32[4,2,216,128]{3,2,1,0:T(8,128)}, u32[]{:S(2)}, u32[]{:S(2)}) async-start(f32[4,2,216,128]{3,2,1,0:T(8,128)} %bitcast.7), calls=%async_computation.1 | async-start | bytes 1769472 | tf_op jit(solution)/shard_map/all_to_all | solution.py:314
  37.0 7.2 %collective-permute-done.1 = f32[8,216,128]{2,1,0:T(8,128)S(1)} collective-permute-done((f32[8,216,128]{2,1,0:T(8,128)S(1)}, f32[8,216,128]{2,1,0:T(8,128)S(1)}, u32[]{:S(2)}, u32[]{:S(2)}) %collective-permute-start.1) | collective-permute-done | bytes 884768 | tf_op jit(solution)/shard_map/ppermute | solution.py:302
  44.2 6.1 %collective-permute-done = f32[8,216,128]{2,1,0:T(8,128)S(1)} collective-permute-done((f32[8,216,128]{2,1,0:T(8,128)S(1)}, f32[8,216,128]{2,1,0:T(8,128)S(1)}, u32[]{:S(2)}, u32[]{:S(2)}) %collective-permute-start) | collective-permute-done | bytes 884768 | tf_op jit(solution)/shard_map/ppermute | solution.py:302
  51.2 1.6 %pad_maximum_fusion = f32[3,8,216,128]{3,2,1,0:T(8,128)S(1)} fusion(f32[1,8,216,128]{3,2,1,0:T(8,128)} %bitcast.46, f32[1,8,216,128]{3,2,1,0:T(8,128)} %bitcast.47, f32[1,8,216,128]{3,2,1,0:T(8,128)S(1)} %bitcast.39), kind=kLoop, calls=%fused_computation.5 | loop fusion | flops 1327104 | bytes 5308416 | tf_op jit(solution)/shard_map/stack | solution.py:310
  52.8 1.5 gather_fusion.4
  54.4 4.4 %all-to-all-start.2 = ((f32[4,2,216,128]{3,2,1,0:T(8,128)}), f32[4,2,216,128]{3,2,1,0:T(8,128)}, u32[]{:S(2)}, u32[]{:S(2)}) async-start(f32[4,2,216,128]{3,2,1,0:T(8,128)} %bitcast.44), calls=%async_computation.2 | async-start | bytes 1769472 | tf_op jit(solution)/shard_map/all_to_all | solution.py:315
  59.5 2.4 %slice.61 = f32[47,48,48]{2,1,0:T(8,128)S(1)} reverse(f32[47,48,48]{2,1,0:T(8,128)S(1)} %slice.60), dimensions={0,1,2} | reverse | bytes 866304 | tf_op jit(solution)/shard_map/jit(_roll_static)/slice | solution.py:61
  65.3 2.2 %fusion.2 = f32[25,48,48]{2,1,0:T(8,128)} fusion(f32[25,48,48]{2,1,0:T(8,128)} %slice.55, f32[48,48,47]{2,1,0:T(8,128)S(1)} %bitcast.42, f32[48,48,1]{2,1,0:T(8,128)S(1)} %slice.80, f32[25]{0:T(128)S(1)} %copy-done.9), kind=kLoop, calls=%fused_computation.14 | loop fusion | flops 172800 | bytes 903268 | tf_op jit(solution)/shard_map/mul | solution.py:65
  70.8 9.5 %pair_terms.1 = f32[2,2,864,128]{3,2,1,0:T(8,128)} custom-call(f32[4,2,216,128]{3,2,1,0:T(8,128)} %all-to-all-done.1.first_ref, f32[4,2,216,128]{3,2,1,0:T(8,128)} %all-to-all-done.2.second_ref, f32[152,384]{1,0:T(8,128)} %pad.4.modes_ref, bf16[304,864]{1,0:T(8,128)(2,1)} %constant.28.clone.fwd_left, bf16[288,912]{1,0:T(8,128)(2,1)} %constant.29.clone.inv_left, ...), custom_call_target="tpu_custom_call" | custom-call | tf_op jit(solution)/shard_map/pair_terms/pallas_call | solution.py:183
  80.2 2.8 %copy.28 = f32[2,2,4,216,128]{4,3,1,0,2:T(8,128)} copy(f32[2,2,4,216,128]{4,3,2,1,0:T(8,128)} %bitcast.43) | data formatting | bytes 3538944 | tf_op jit(solution)/shard_map/reshape | solution.py:317
  83.1 4.2 %all-to-all-start.3 = ((f32[2,2,4,216,128]{4,3,1,0,2:T(8,128)}), f32[2,2,4,216,128]{4,3,1,0,2:T(8,128)S(1)}, u32[]{:S(2)}, u32[]{:S(2)}) async-start(f32[2,2,4,216,128]{4,3,1,0,2:T(8,128)} %copy.28), calls=%async_computation.3 | async-start | bytes 3538944 | tf_op jit(solution)/shard_map/all_to_all | solution.py:318
  87.9 15.3 %all-to-all-done.3 = f32[2,2,4,216,128]{4,3,1,0,2:T(8,128)S(1)} async-done(((f32[2,2,4,216,128]{4,3,1,0,2:T(8,128)}), f32[2,2,4,216,128]{4,3,1,0,2:T(8,128)S(1)}, u32[]{:S(2)}, u32[]{:S(2)}) %all-to-all-start.3) | async-done | bytes 1769504 | tf_op jit(solution)/shard_map/all_to_all | solution.py:318
  104.4 8.8 %collective-permute-start.2 = (f32[8,216,128]{2,1,0:T(8,128)S(1)}, f32[8,216,128]{2,1,0:T(8,128)S(1)}, u32[]{:S(2)}, u32[]{:S(2)}) collective-permute-start(f32[8,216,128]{2,1,0:T(8,128)S(1)} %get-tuple-element.13), channel_id=1, source_target_pairs={{252,0},{0,4},{4,8},{8,12},{12,16},{16,20},{20,24},{24,28},{28,32}... | collective-permute-start | bytes 2654216 | tf_op jit(solution)/shard_map/ppermute | solution.py:302
  113.2 1.7 %collective-permute-start.3 = (f32[8,216,128]{2,1,0:T(8,128)S(1)}, f32[8,216,128]{2,1,0:T(8,128)S(1)}, u32[]{:S(2)}, u32[]{:S(2)}) collective-permute-start(f32[8,216,128]{2,1,0:T(8,128)S(1)} %get-tuple-element.12), channel_id=1, source_target_pairs={{248,0},{252,4},{0,8},{4,12},{8,16},{12,20},{16,24},{20,28},{24,32... | collective-permute-start | bytes 2654216 | tf_op jit(solution)/shard_map/ppermute | solution.py:302
  114.9 16.9 %collective-permute-done.2.one_ref = f32[8,216,128]{2,1,0:T(8,128)S(1)} collective-permute-done((f32[8,216,128]{2,1,0:T(8,128)S(1)}, f32[8,216,128]{2,1,0:T(8,128)S(1)}, u32[]{:S(2)}, u32[]{:S(2)}) %collective-permute-start.2) | collective-permute-done | bytes 884768 | tf_op jit(solution)/shard_map/ppermute | solution.py:302
  131.8 17.1 %collective-permute-done.3.two_ref = f32[8,216,128]{2,1,0:T(8,128)S(1)} collective-permute-done((f32[8,216,128]{2,1,0:T(8,128)S(1)}, f32[8,216,128]{2,1,0:T(8,128)S(1)}, u32[]{:S(2)}, u32[]{:S(2)}) %collective-permute-start.3) | collective-permute-done | bytes 884768 | tf_op jit(solution)/shard_map/ppermute | solution.py:302
  148.9 4.1 %correlated.1 = (f32[8,216,128]{2,1,0:T(8,128)S(1)}, f32[8,128]{1,0:T(8,128)S(1)}) custom-call(f32[8,216,128]{2,1,0:T(8,128)S(1)} %bitcast.40, f32[8,216,128]{2,1,0:T(8,128)S(1)} %get-tuple-element.14.own_ref, f32[8,216,128]{2,1,0:T(8,128)S(1)} %collective-permute-done.2.one_ref, f32[8,216,128]{2,1,0:T(8,128)S(1)} %collective-permute-done.3.two_ref), custom_call_target="tpu_custom_call" | custom-call | tf_op jit(solution)/shard_map/correlated/pallas_call | solution.py:257
  153.0 1.6 %projected.1 = (f32[8,12,2304]{2,1,0:T(8,128)S(1)}, f32[1,8,8]{2,1,0:T(8,128)}) custom-call(f32[8,216,128]{2,1,0:T(8,128)S(1)} %bitcast.41, f32[8,216,128]{2,1,0:T(8,128)S(1)} %get-tuple-element.4.action_ref, f32[8,128]{1,0:T(8,128)S(1)} %get-tuple-element.5.total_ref), custom_call_target="tpu_custom_call" | custom-call | tf_op jit(solution)/shard_map/projected/pallas_call | solution.py:289
  154.5 1.4 copy.30
  (48 shorter events, 11.5 us)
Async XLA Ops:
  1.9 27.2 %copy-start.8 = (s32[8]{0:T(128)S(1)}, s32[8]{0:T(128)}, u32[]{:S(2)}) copy-start(s32[8]{0:T(128)} %constant.55) | copy-start | bytes 100
  1.9 27.2 %copy-start.2 = (s32[8]{0:T(128)S(1)}, s32[8]{0:T(128)}, u32[]{:S(2)}) copy-start(s32[8]{0:T(128)} %first.1) | copy-start | bytes 100
  19.2 25.0 %collective-permute-start.1 = (f32[8,216,128]{2,1,0:T(8,128)S(1)}, f32[8,216,128]{2,1,0:T(8,128)S(1)}, u32[]{:S(2)}, u32[]{:S(2)}) collective-permute-start(f32[8,216,128]{2,1,0:T(8,128)S(1)} %bitcast.36), channel_id=1, source_target_pairs={{8,0},{12,4},{16,8},{20,12},{24,16},{28,20},{32,24},{36,28},{40,32... | collective-permute-start | bytes 2654216 | tf_op jit(solution)/shard_map/ppermute | solution.py:302
  27.0 23.3 %collective-permute-start = (f32[8,216,128]{2,1,0:T(8,128)S(1)}, f32[8,216,128]{2,1,0:T(8,128)S(1)}, u32[]{:S(2)}, u32[]{:S(2)}) collective-permute-start(f32[8,216,128]{2,1,0:T(8,128)S(1)} %bitcast.37), channel_id=1, source_target_pairs={{4,0},{8,4},{12,8},{16,12},{20,16},{24,20},{28,24},{32,28},{36,32}... | collective-permute-start | bytes 2654216 | tf_op jit(solution)/shard_map/ppermute | solution.py:302
  31.3 4.4 %copy-start = (s32[8]{0:T(128)S(1)}, s32[8]{0:T(128)}, u32[]{:S(2)}) copy-start(s32[8]{0:T(128)} %reach.1) | copy-start | bytes 100
  31.3 5.0 %copy-start.3 = (s32[8]{0:T(128)S(1)}, s32[8]{0:T(128)}, u32[]{:S(2)}) copy-start(s32[8]{0:T(128)} %second.1) | copy-start | bytes 100
  31.3 23.1 %all-to-all-start.1 = ((f32[4,2,216,128]{3,2,1,0:T(8,128)}), f32[4,2,216,128]{3,2,1,0:T(8,128)}, u32[]{:S(2)}, u32[]{:S(2)}) async-start(f32[4,2,216,128]{3,2,1,0:T(8,128)} %bitcast.7), calls=%async_computation.1 | async-start | bytes 1769472 | tf_op jit(solution)/shard_map/all_to_all | solution.py:314
  44.2 6.1 %copy-start.5 = (f32[8,216,128]{2,1,0:T(8,128)}, f32[8,216,128]{2,1,0:T(8,128)S(1)}, u32[]{:S(2)}) copy-start(f32[8,216,128]{2,1,0:T(8,128)S(1)} %collective-permute-done.1) | copy-start | bytes 2654212
  50.3 1.0 copy-start.6
  54.4 4.4 %copy-start.4 = (f32[48,2304]{1,0:T(8,128)S(1)}, f32[48,2304]{1,0:T(8,128)}, u32[]{:S(2)}) copy-start(f32[48,2304]{1,0:T(8,128)} %param.17) | copy-start | bytes 1327108
  54.4 16.4 %all-to-all-start.2 = ((f32[4,2,216,128]{3,2,1,0:T(8,128)}), f32[4,2,216,128]{3,2,1,0:T(8,128)}, u32[]{:S(2)}, u32[]{:S(2)}) async-start(f32[4,2,216,128]{3,2,1,0:T(8,128)} %bitcast.44), calls=%async_computation.2 | async-start | bytes 1769472 | tf_op jit(solution)/shard_map/all_to_all | solution.py:315
  63.2 1.0 slice-start
  63.2 2.2 %copy-start.9 = (f32[25]{0:T(128)S(1)}, f32[25]{0:T(128)}, u32[]{:S(2)}) copy-start(f32[25]{0:T(128)} %constant.41) | copy-start | bytes 304
  68.7 0.7 copy-start.7
  83.1 20.1 %all-to-all-start.3 = ((f32[2,2,4,216,128]{4,3,1,0,2:T(8,128)}), f32[2,2,4,216,128]{4,3,1,0,2:T(8,128)S(1)}, u32[]{:S(2)}, u32[]{:S(2)}) async-start(f32[2,2,4,216,128]{4,3,1,0,2:T(8,128)} %copy.28), calls=%async_computation.3 | async-start | bytes 3538944 | tf_op jit(solution)/shard_map/all_to_all | solution.py:318
  87.9 15.4 %copy-start.1 = (s32[8]{0:T(128)S(1)}, s32[8]{0:T(128)}, u32[]{:S(2)}) copy-start(s32[8]{0:T(128)} %reach.1) | copy-start | bytes 100
  104.4 27.4 %collective-permute-start.2 = (f32[8,216,128]{2,1,0:T(8,128)S(1)}, f32[8,216,128]{2,1,0:T(8,128)S(1)}, u32[]{:S(2)}, u32[]{:S(2)}) collective-permute-start(f32[8,216,128]{2,1,0:T(8,128)S(1)} %get-tuple-element.13), channel_id=1, source_target_pairs={{252,0},{0,4},{4,8},{8,12},{12,16},{16,20},{20,24},{24,28},{28,32}... | collective-permute-start | bytes 2654216 | tf_op jit(solution)/shard_map/ppermute | solution.py:302
  113.2 35.7 %collective-permute-start.3 = (f32[8,216,128]{2,1,0:T(8,128)S(1)}, f32[8,216,128]{2,1,0:T(8,128)S(1)}, u32[]{:S(2)}, u32[]{:S(2)}) collective-permute-start(f32[8,216,128]{2,1,0:T(8,128)S(1)} %get-tuple-element.12), channel_id=1, source_target_pairs={{248,0},{252,4},{0,8},{4,12},{8,16},{12,20},{16,24},{20,28},{24,32... | collective-permute-start | bytes 2654216 | tf_op jit(solution)/shard_map/ppermute | solution.py:302

commit v2 on v1

v2 whole, which is shorter than its diff:
```python
import functools
import math

import jax
import jax.numpy as jnp
import ml_dtypes
import numpy as np
from jax import lax
from jax.experimental import pallas as pl
from jax.experimental.pallas import tpu as pltpu
from jax.sharding import PartitionSpec as P

MESH = pl.DeviceIdType.MESH
B = 48
FRAG = 8
GRP = 4
TURNS = 2
TILES = 18
SLAB = 216
ROWS = 864
HALF = 25
CH = 152
PADX = 16
PADT = 8
CHUNKS = 3
CHUNK = SLAB // CHUNKS


def split(a):
    a = a.astype(np.float32)
    head = a.astype(ml_dtypes.bfloat16)
    tail = (a - head.astype(np.float32)).astype(ml_dtypes.bfloat16)
    return head, tail


@functools.lru_cache(None)
def tables():
    c, kx = np.meshgrid(np.arange(6), np.arange(HALF), indexing="ij")
    c, kx = c.reshape(-1, 1), kx.reshape(-1, 1)
    a, x = np.meshgrid(np.arange(6), np.arange(B), indexing="ij")
    a, x = a.reshape(1, -1), x.reshape(1, -1)
    theta = 2 * np.pi * ((8 * c * a + kx * x) % 48) / 48
    left = np.zeros((2 * CH, 288))
    left[:150] = np.cos(theta)
    left[CH:CH + 150] = -np.sin(theta)
    left = np.concatenate(split(left), axis=1)
    inverse = np.concatenate([left[:, :288].T, left[:, 288:].T], axis=1)
    b, z = np.meshgrid(np.arange(8), np.arange(B), indexing="ij")
    b, z = b.reshape(-1), z.reshape(-1)
    phi = 2 * np.pi * ((6 * np.outer(b, b) + np.outer(z, z)) % 48) / 48
    right = np.concatenate(split(np.concatenate([np.cos(phi), -np.sin(phi)], axis=1)), axis=0)
    turn = 2 * np.pi * ((np.arange(6)[:, None] * b[None, :]) % 48) / 48
    twiddle = np.stack([np.cos(turn), -np.sin(turn)]).astype(np.float32)
    return left, inverse, right, twiddle


def halves(value):
    head = value.astype(jnp.bfloat16)
    return head, (value - head.astype(jnp.float32)).astype(jnp.bfloat16)


def dot(a, b):
    return jnp.dot(a, b, preferred_element_type=jnp.float32)


def modes_kernel(kernel_ref, modes_ref, picked, mirrored):
    for c in range(6):
        for e in range(8):
            picked[48 * c:48 * c + 48, 48 * e:48 * e + 48] = kernel_ref[:, 48 * (c + 6 * e):48 * (c + 6 * e) + 48]
    lane = lax.broadcasted_iota(jnp.int32, (1, 384), 1)
    e, kz = lane // B, lane % B
    row = lax.broadcasted_iota(jnp.int32, (384, 384), 0)
    for shift, rows in ((0, slice(0, 48)), (1, slice(48, 288))):
        source = (16 - e - shift) % 8 * B + (B - kz) % B
        permute = jnp.where(row == source, 1.0, 0.0).astype(jnp.bfloat16)
        head, tail = halves(picked[rows, :])
        mirrored[rows, :] = dot(head, permute) + dot(tail, permute)
    out = lax.broadcasted_iota(jnp.int32, (32, B), 0)
    permute = jnp.where(lax.broadcasted_iota(jnp.int32, (32, B), 1) == (B - out) % B, 1.0, 0.0).astype(jnp.bfloat16)
    kx = lax.broadcasted_iota(jnp.int32, (32, 384), 0)
    weight = jnp.where((kx == 0) | (kx == HALF - 1), 0.5 / B**3, 1.0 / B**3)
    modes_ref[144:CH, :] = jnp.zeros((8, 384), jnp.float32)
    for c in range(6):
        other = (6 - c) % 6
        head, tail = halves(mirrored[48 * other:48 * other + 48, :])
        even = (picked[48 * c:48 * c + 32, :] + dot(permute, head) + dot(permute, tail)) * weight
        modes_ref[HALF * c:HALF * c + HALF, :] = even[:HALF]


def mode_table(kernel):
    vmem = pl.BlockSpec(memory_space=pltpu.VMEM)
    return pl.pallas_call(
        modes_kernel,
        out_shape=jax.ShapeDtypeStruct((CH, 384), jnp.float32),
        in_specs=[vmem],
        out_specs=vmem,
        scratch_shapes=[pltpu.VMEM((288, 384), jnp.float32), pltpu.VMEM((288, 384), jnp.float32)],
        compiler_params=pltpu.CompilerParams(vmem_limit_bytes=40 << 20),
        name="mode_table",
    )(kernel)


def shifted(source, offset, emit):
    d0, d1, d2 = offset
    flat = 48 * d1 + d2 + 1024
    tile = lax.shift_right_logical(flat, 7) - 8
    lane_by = lax.bitwise_and(flat, 127)
    lane = lax.broadcasted_iota(jnp.int32, (B, 128), 1)
    late = lane >= lane_by
    insides = []
    for k in range(3):
        z = lax.rem(lane + 128 * k, B) - d2
        insides.append((z >= 0) & (z < B))
    before = None
    for t in range(-1, TILES):
        block = source[t - tile + PADT, pl.ds(PADX - d0, B), :]
        block = pltpu.roll(block, lane_by, 1)
        if t >= 0:
            emit(t, jnp.where(insides[t % 3], jnp.where(late, block, before), 0.0))
        before = block


def pair_kernel(pairs_ref, modes_ref, left_ref, inverse_ref, right_ref, twiddle_ref, anchors, reach_ref,
                out_ref, padded, moved, stack, wide, spec, volume, left, inverse, right, twiddle):
    left[:, 0:288] = left_ref[:, 0:288]
    left[:, 288:864] = left_ref[...]
    inverse[:, 0:304] = inverse_ref[:, 0:304]
    inverse[:, 304:912] = inverse_ref[...]
    right[0:384, :] = right_ref[0:384, :]
    right[384:1152, :] = right_ref[...]
    for c in range(6):
        rows = slice(HALF * c, HALF * c + HALF + 2 * (c == 5))
        for part in range(2):
            twiddle[part, rows, :] = jnp.broadcast_to(twiddle_ref[part, c:c + 1, :], (rows.stop - rows.start, 384))
    frag, member = lax.axis_index("orb"), lax.axis_index("grp")

    def offset_of(turn):
        partner = lax.rem(frag + reach_ref[member + GRP * turn], lax.axis_size("orb"))
        return [anchors[partner, k] - anchors[frag, k] for k in range(3)]

    padded[...] = jnp.zeros_like(padded)

    def at(t):
        return slice(48 * (t // 3), 48 * (t // 3) + 48), slice(128 * (t % 3), 128 * (t % 3) + 128)

    for turn in range(TURNS):
        for t in range(TILES):
            padded[t + PADT, pl.ds(PADX, B), :] = pairs_ref[turn, 1, pl.ds(t, B, stride=TILES), :]

        def emit(t, block):
            moved[turn, t] = block
            density = pairs_ref[turn, 0, pl.ds(t, B, stride=TILES), :] * block
            head, tail = halves(density)
            rows, lanes = at(t)
            lanes = slice(384 * turn + lanes.start, 384 * turn + lanes.stop)
            stack[rows.start:rows.stop, lanes] = head
            stack[288 + rows.start:288 + rows.stop, lanes] = tail
            stack[576 + rows.start:576 + rows.stop, lanes] = head

        shifted(padded, offset_of(turn), emit)

    volume[0:2 * CH, :] = dot(left[...], stack[0:864, :])
    tr, ti = twiddle[0], twiddle[1]

    def put(row, value):
        head, tail = halves(value)
        wide[row:row + CH, 0:384] = head
        wide[row:row + CH, 384:768] = tail
        wide[row:row + CH, 768:1152] = head

    for turn in range(TURNS):
        re = volume[0:CH, 384 * turn:384 * turn + 384]
        im = volume[CH:2 * CH, 384 * turn:384 * turn + 384]
        put(2 * CH * turn, re * tr - im * ti)
        put(2 * CH * turn + CH, re * ti + im * tr)
    spec[...] = dot(wide[...], right[...])
    table = modes_ref[...]
    for turn in range(TURNS):
        row = 2 * CH * turn
        re = spec[row:row + CH, 0:384] - spec[row + CH:row + 2 * CH, 384:768]
        im = spec[row:row + CH, 384:768] + spec[row + CH:row + 2 * CH, 0:384]
        put(row, re * table)
        put(row + CH, im * table)
    spec[...] = dot(wide[...], right[...])
    for turn in range(TURNS):
        row = 2 * CH * turn
        re = spec[row:row + CH, 0:384] + spec[row + CH:row + 2 * CH, 384:768]
        im = spec[row + CH:row + 2 * CH, 0:384] - spec[row:row + CH, 384:768]
        lanes = slice(384 * turn, 384 * turn + 384)
        for part, value in enumerate((re * tr + im * ti, im * tr - re * ti)):
            head, tail = halves(value)
            stack[CH * part:CH * part + CH, lanes] = head
            stack[304 + CH * part:304 + CH * part + CH, lanes] = tail
            stack[608 + CH * part:608 + CH * part + CH, lanes] = head
    volume[0:288, :] = dot(inverse[...], stack[...])

    for turn in range(TURNS):
        for t in range(TILES):
            rows, lanes = at(t)
            potential = volume[rows, 384 * turn + lanes.start:384 * turn + lanes.stop]
            out_ref[turn, 0, pl.ds(t, B, stride=TILES), :] = potential * moved[turn, t]
            padded[t + PADT, pl.ds(PADX, B), :] = potential * pairs_ref[turn, 0, pl.ds(t, B, stride=TILES), :]

        def emit(t, block):
            out_ref[turn, 1, pl.ds(t, B, stride=TILES), :] = block

        shifted(padded, [-d for d in offset_of(turn)], emit)


def pair_terms(pairs, modes, anchors, reach):
    left, inverse, right, twiddle = tables()
    vmem, smem = pl.BlockSpec(memory_space=pltpu.VMEM), pl.BlockSpec(memory_space=pltpu.SMEM)
    return pl.pallas_call(
        pair_kernel,
        out_shape=jax.ShapeDtypeStruct((TURNS, 2, ROWS, 128), jnp.float32),
        in_specs=[vmem] * 6 + [smem] * 2,
        out_specs=vmem,
        scratch_shapes=[
            pltpu.VMEM((TILES + 2 * PADT, B + 2 * PADX, 128), jnp.float32),
            pltpu.VMEM((TURNS, TILES, B, 128), jnp.float32),
            pltpu.VMEM((912, 768), jnp.bfloat16),
            pltpu.VMEM((2 * TURNS * CH, 1152), jnp.bfloat16),
            pltpu.VMEM((2 * TURNS * CH, 768), jnp.float32),
            pltpu.VMEM((2 * CH, 768), jnp.float32),
            pltpu.VMEM((2 * CH, 864), jnp.bfloat16),
            pltpu.VMEM((288, 912), jnp.bfloat16),
            pltpu.VMEM((1152, 768), jnp.bfloat16),
            pltpu.VMEM((2, CH, 384), jnp.float32),
        ],
        compiler_params=pltpu.CompilerParams(vmem_limit_bytes=56 << 20),
        name="pair_terms",
    )(pairs, modes, jnp.asarray(left), jnp.asarray(inverse), jnp.asarray(right), jnp.asarray(twiddle), anchors, reach)


def sibling(orb):
    return orb + 1 - 2 * lax.rem(orb, 2)


def greet(orb, member):
    barrier = pltpu.get_barrier_semaphore()
    orbs = lax.axis_size("orb")
    for step in range(1, GRP):
        pl.semaphore_signal(barrier, inc=1, device_id={"grp": lax.rem(member + step, GRP)}, device_id_type=MESH)
    for other in (sibling(orb), lax.rem(orb + 2, orbs), lax.rem(orb + orbs - 2, orbs)):
        pl.semaphore_signal(barrier, inc=1, device_id={"orb": other}, device_id_type=MESH)
    pl.semaphore_wait(barrier, GRP - 1 + 3)


def spread_kernel(mine, first, second, reach, phi_ref, pairs_ref, *scratch):
    near = scratch[0:3 * CHUNKS]
    out = scratch[3 * CHUNKS:5 * CHUNKS]
    send_slab, recv_slab, own_sem, send_ahead, recv_ahead, send_side, recv_side, send_pick, recv_pick = scratch[5 * CHUNKS:]
    orb, me = lax.axis_index("orb"), lax.axis_index("grp")
    orbs = lax.axis_size("orb")
    even = lax.rem(orb, 2) == 0
    behind = lax.rem(orb + orbs - 2, orbs)
    greet(orb, me)

    def rows(c):
        return pl.ds(CHUNK * c, CHUNK)

    slabs, owns = [], []
    for c in range(CHUNKS):
        group = []
        for step in (2, 1, 3):
            other = lax.rem(me + step, GRP)
            group.append(pltpu.make_async_remote_copy(
                src_ref=mine.at[:, other, rows(c)], dst_ref=near[3 * c].at[pl.ds(2 * me, 2)],
                send_sem=send_slab.at[c, step], recv_sem=recv_slab.at[c, step],
                device_id={"grp": other}, device_id_type=MESH))
        slabs.append(group)
        owns.append(pltpu.make_async_copy(mine.at[:, me, rows(c)], near[3 * c].at[pl.ds(2 * me, 2)], own_sem.at[c]))
        owns[c].start()
        for copy in group:
            copy.start()

    ahead = [pltpu.make_async_remote_copy(
        src_ref=near[3 * c], dst_ref=near[3 * c + 2], send_sem=send_ahead.at[c], recv_sem=recv_ahead.at[c],
        device_id={"orb": behind}, device_id_type=MESH) for c in range(CHUNKS)]
    side = [[pltpu.make_async_remote_copy(
        src_ref=near[3 * c + which], dst_ref=near[3 * c + 1], send_sem=send_side.at[c], recv_sem=recv_side.at[c],
        device_id={"orb": sibling(orb)}, device_id_type=MESH) for which in (2, 0)] for c in range(CHUNKS)]

    def picks(which, c):
        copies = []
        for step in (2, 1, 3):
            other = lax.rem(me + step, GRP)
            copies.append(pltpu.make_async_remote_copy(
                src_ref=out[2 * c + which].at[other],
                dst_ref=pairs_ref.at[:, which, pl.ds(SLAB * me + CHUNK * c, CHUNK)],
                send_sem=send_pick.at[which, c, step], recv_sem=recv_pick.at[which, c, step],
                device_id={"grp": other}, device_id_type=MESH))
        return copies

    picked = [[picks(which, c) for c in range(CHUNKS)] for which in range(2)]

    def choose(which, c):
        for slot in range(GRP * TURNS):
            if which == 0:
                value = near[3 * c][first[slot]]
            else:
                value = near[3 * c][second[slot]]
                value = jnp.where(reach[slot] == 1, near[3 * c + 1][second[slot]], value)
                value = jnp.where(reach[slot] == 2, near[3 * c + 2][second[slot]], value)
            out[2 * c + which][slot % GRP, slot // GRP] = value
        for copy in picked[which][c]:
            copy.start()
        pairs_ref[:, which, pl.ds(pl.multiple_of(SLAB * me + CHUNK * c, 8), CHUNK), :] = out[2 * c + which][me]

    for c in range(CHUNKS):
        owns[c].wait()
        for copy in slabs[c]:
            copy.wait_recv()
        ahead[c].start()

        @pl.when(jnp.logical_not(even))
        def _():
            side[c][1].start()

        choose(0, c)
        phi_ref[:, CHUNK * c:CHUNK * c + CHUNK, :] = near[3 * c][...]
    for c in range(CHUNKS + 1):
        if c < CHUNKS:
            ahead[c].wait_recv()

            @pl.when(even)
            def _():
                side[c][0].start()

        if c > 0:
            side[c - 1][0].wait_recv()
            choose(1, c - 1)
    for c in range(CHUNKS):
        for copy in slabs[c]:
            copy.wait_send()
        ahead[c].wait_send()

        @pl.when(even)
        def _():
            side[c][0].wait_send()

        @pl.when(jnp.logical_not(even))
        def _():
            side[c][1].wait_send()

        for which in range(2):
            for copy in picked[which][c]:
                copy.wait()


def spread(mine, first, second, reach):
    vmem, smem = pl.BlockSpec(memory_space=pltpu.VMEM), pl.BlockSpec(memory_space=pltpu.SMEM)
    dma = pltpu.SemaphoreType.DMA
    return pl.pallas_call(
        spread_kernel,
        out_shape=(jax.ShapeDtypeStruct((FRAG, SLAB, 128), jnp.float32),
                   jax.ShapeDtypeStruct((TURNS, 2, ROWS, 128), jnp.float32)),
        in_specs=[vmem] + [smem] * 3,
        out_specs=(vmem, vmem),
        scratch_shapes=[pltpu.VMEM((FRAG, CHUNK, 128), jnp.float32)] * (3 * CHUNKS)
        + [pltpu.VMEM((GRP, TURNS, CHUNK, 128), jnp.float32)] * (2 * CHUNKS)
        + [dma((CHUNKS, GRP)), dma((CHUNKS, GRP)), dma((CHUNKS,)), dma((CHUNKS,)), dma((CHUNKS,)),
           dma((CHUNKS,)), dma((CHUNKS,)), dma((2, CHUNKS, GRP)), dma((2, CHUNKS, GRP))],
        compiler_params=pltpu.CompilerParams(collective_id=0, has_side_effects=True, vmem_limit_bytes=40 << 20),
        name="spread",
    )(mine, first, second, reach)


def collect_kernel(terms, phi_ref, count, first, second, reach, action_ref, total_ref, *scratch):
    landed = scratch[0:CHUNKS]
    aside = scratch[CHUNKS:2 * CHUNKS]
    beside = scratch[2 * CHUNKS:3 * CHUNKS]
    onward = scratch[3 * CHUNKS:4 * CHUNKS]
    behind = scratch[4 * CHUNKS:5 * CHUNKS]
    (products, block, blocks, send_term, recv_term, send_side, recv_side, send_on, recv_on,
     send_sum, recv_sum) = scratch[5 * CHUNKS:]
    orb, me = lax.axis_index("orb"), lax.axis_index("grp")
    orbs = lax.axis_size("orb")
    even = jnp.where(lax.rem(orb, 2) == 0, 1.0, 0.0)
    greet(orb, me)

    def rows(c):
        return pl.ds(CHUNK * c, CHUNK)

    moved = []
    for c in range(CHUNKS):
        group = []
        for step in (2, 1, 3):
            other = lax.rem(me + step, GRP)
            group.append(pltpu.make_async_remote_copy(
                src_ref=terms.at[:, :, other, rows(c)], dst_ref=landed[c].at[me],
                send_sem=send_term.at[c, step], recv_sem=recv_term.at[c, step],
                device_id={"grp": other}, device_id_type=MESH))
        moved.append(group)
        for copy in group:
            copy.start()
    side = [pltpu.make_async_remote_copy(
        src_ref=aside[c], dst_ref=beside[c], send_sem=send_side.at[c], recv_sem=recv_side.at[c],
        device_id={"orb": sibling(orb)}, device_id_type=MESH) for c in range(CHUNKS)]
    on = [pltpu.make_async_remote_copy(
        src_ref=onward[c], dst_ref=behind[c], send_sem=send_on.at[c], recv_sem=recv_on.at[c],
        device_id={"orb": lax.rem(orb + 2, orbs)}, device_id_type=MESH) for c in range(CHUNKS)]
    live = [jnp.where(slot < count[0], 1.0, 0.0) for slot in range(GRP * TURNS)]

    def summed(c, a, which, far):
        value = jnp.zeros((CHUNK, 128), jnp.float32)
        for slot in range(GRP * TURNS):
            term = landed[c][slot % GRP, slot // GRP, which]
            if which == 0:
                weight = jnp.where(first[slot] == a, live[slot], 0.0)
            else:
                weight = jnp.where((second[slot] == a) & (reach[slot] == far), live[slot], 0.0)
            value = value + weight * term
        return value

    for c in range(CHUNKS):
        landed[c][me] = terms[:, :, me, rows(c)]
    for c in range(CHUNKS):
        for copy in moved[c]:
            copy.wait_recv()
        for a in range(FRAG):
            aside[c][a] = summed(c, a, 1, 1)
        side[c].start()
        for a in range(FRAG):
            onward[c][a] = summed(c, a, 1, 2)
            action_ref[a, CHUNK * c:CHUNK * c + CHUNK, :] = summed(c, a, 0, 0) + summed(c, a, 1, 0)
        side[c].wait_recv()
        for a in range(FRAG):
            onward[c][a] = onward[c][a] + even * beside[c][a]
        on[c].start()
    products[...] = jnp.zeros_like(products)
    for c in range(CHUNKS):
        on[c].wait_recv()
        for b in range(FRAG):
            value = action_ref[b, CHUNK * c:CHUNK * c + CHUNK, :] + behind[c][b] + (1.0 - even) * beside[c][b]
            action_ref[b, CHUNK * c:CHUNK * c + CHUNK, :] = value
            for a in range(FRAG):
                part = jnp.sum((phi_ref[a, CHUNK * c:CHUNK * c + CHUNK, :] * value).reshape(CHUNK // 8, 8, 128), axis=0)
                products[b, a] = products[b, a] + part
    lane = lax.broadcasted_iota(jnp.int32, (FRAG, 128), 1)
    total = jnp.zeros((FRAG, 128), jnp.float32)
    for b in range(FRAG):
        part = jnp.sum(jnp.sum(products[b], axis=1), axis=1, keepdims=True)
        total = total + jnp.where(lane == b, part, 0.0)
    block[...] = total
    sums = []
    for step in range(1, GRP):
        sums.append(pltpu.make_async_remote_copy(
            src_ref=block, dst_ref=blocks.at[step], send_sem=send_sum.at[step], recv_sem=recv_sum.at[step],
            device_id={"grp": lax.rem(me + step, GRP)}, device_id_type=MESH))
        sums[-1].start()
    for c in range(CHUNKS):
        for copy in moved[c] + [side[c], on[c]]:
            copy.wait_send()
    for copy in sums:
        copy.wait()
    total_ref[...] = ((block[...] + blocks[2]) + (blocks[1] + blocks[3])) / float(B**3)


def collect(terms, phi, count, first, second, reach):
    vmem, smem = pl.BlockSpec(memory_space=pltpu.VMEM), pl.BlockSpec(memory_space=pltpu.SMEM)
    dma = pltpu.SemaphoreType.DMA
    return pl.pallas_call(
        collect_kernel,
        out_shape=(jax.ShapeDtypeStruct((FRAG, SLAB, 128), jnp.float32),
                   jax.ShapeDtypeStruct((FRAG, 128), jnp.float32)),
        in_specs=[vmem] * 2 + [smem] * 4,
        out_specs=(vmem, vmem),
        scratch_shapes=[pltpu.VMEM((GRP, TURNS, 2, CHUNK, 128), jnp.float32)] * CHUNKS
        + [pltpu.VMEM((FRAG, CHUNK, 128), jnp.float32)] * (4 * CHUNKS)
        + [pltpu.VMEM((FRAG, FRAG, 8, 128), jnp.float32),
           pltpu.VMEM((FRAG, 128), jnp.float32),
           pltpu.VMEM((GRP, FRAG, 128), jnp.float32),
           dma((CHUNKS, GRP)), dma((CHUNKS, GRP)), dma((CHUNKS,)), dma((CHUNKS,)), dma((CHUNKS,)), dma((CHUNKS,)),
           dma((GRP,)), dma((GRP,))],
        compiler_params=pltpu.CompilerParams(collective_id=1, has_side_effects=True, vmem_limit_bytes=40 << 20),
        name="collect",
    )(terms, phi, count, first, second, reach)


def project_kernel(phi_ref, action_ref, total_ref, gradient_ref, lagrange_ref, flat):
    total = total_ref[...][:, 0:FRAG]
    lagrange = 0.5 * (total + total.T)
    lagrange_ref[0] = lagrange
    for a in range(FRAG):
        value = action_ref[a]
        for b in range(FRAG):
            value = value - lagrange[b:b + 1, a:a + 1] * phi_ref[b]
        flat[SLAB * a:SLAB * a + SLAB, :] = value
    for x in range(12):
        for t in range(TILES):
            gradient_ref[FRAG * x:FRAG * x + FRAG, 128 * t:128 * t + 128] = flat[pl.ds(TILES * x + t, FRAG, stride=SLAB), :]


def projected(phi, action, total):
    vmem = pl.BlockSpec(memory_space=pltpu.VMEM)
    return pl.pallas_call(
        project_kernel,
        out_shape=(jax.ShapeDtypeStruct((12 * FRAG, B * B), jnp.float32),
                   jax.ShapeDtypeStruct((1, FRAG, FRAG), jnp.float32)),
        in_specs=[vmem] * 3,
        out_specs=(vmem, vmem),
        scratch_shapes=[pltpu.VMEM((FRAG * SLAB, 128), jnp.float32)],
        compiler_params=pltpu.CompilerParams(vmem_limit_bytes=40 << 20),
        name="projected",
    )(phi, action, total)


def shards(orbitals, kernel, anchors, pair_count, pair_first, pair_second, pair_reach):
    modes = mode_table(kernel)
    mine = orbitals.reshape(2, GRP, SLAB, 128)
    phi, pairs = spread(mine, pair_first, pair_second, pair_reach)
    terms = pair_terms(pairs, modes, anchors, pair_reach).reshape(TURNS, 2, GRP, SLAB, 128)
    action, total = collect(terms, phi, pair_count, pair_first, pair_second, pair_reach)
    gradient, lagrange = projected(phi, action, total)
    return gradient.reshape(12, FRAG, B * B).transpose(1, 0, 2), lagrange


def solution(mesh):
    placed = (P(("orb", "grp"), None, None), P(), P(), P("orb"), P("orb"), P("orb"), P("orb"))
    return jax.shard_map(
        shards,
        mesh=mesh,
        in_specs=placed,
        out_specs=(P("orb", "grp", None), P("orb", None, None)),
        check_vma=False,
    )
```

time: 157 us -> 105 us (0.67)
  Pallas kernels: 16 us -> 98 us
  waiting for transfers between devices: 62.6 us -> 0 us
  starting transfers between devices: 33.3 us -> 0 us
  blocking collectives: 17.3 us -> 0 us
  local copies, waits for them, and re-layouts: 21.4 us -> 5.37 us
  other arithmetic: 3.95 us -> 0 us
    pallas_call x3 -> x4, Pallas kernels: 6.52 us -> 89 us  [the longest x1 43.9 us: collect(): pl.pallas_call(collect_kernel, out_shape=(jax.ShapeDtypeStruct((FRAG, SLA...]
    ppermute x4 -> x0, waiting for transfers between devices: 47.2 us -> none  [passed_along(): lax.ppermute(block, 'orb', [((i - distance) % count, i) for i in range(co...]
    ppermute x4 -> x0, starting transfers between devices: 20.4 us -> none  [passed_along(): lax.ppermute(block, 'orb', [((i - distance) % count, i) for i in range(co...]
    all_to_all x1 -> x0, blocking collectives: 17.3 us -> none  [shards(): lax.all_to_all(orbitals.reshape(2, GRP, SLAB, 128), 'grp', split_axis=1,...]
    all_to_all x3 -> x0, waiting for transfers between devices: 15.3 us -> none  [the longest x1 15.3 us: shards(): lax.all_to_all(terms, 'grp', split_axis=2, concat_axis=2, tiled=True)]
    all_to_all x3 -> x0, starting transfers between devices: 12.9 us -> none  [the longest x1 4.38 us: shards(): lax.all_to_all(first, 'grp', split_axis=0, concat_axis=0, tiled=True)]
    slice x10 -> x0, local copies, waits for them, and re-layouts: 6.38 us -> none  [the longest x7 4.59 us: mode_table(): flipped = jnp.roll(jnp.flip(cube, (0, 1, 2)), (1, 1, 1), (0, 1, 2))]
    gather x5 -> x0, local copies, waits for them, and re-layouts: 4.98 us -> none  [the longest x2 2.16 us: shards(): first = phi[pair_first[order]].reshape(GRP, TURNS, SLAB, 128)]
  transfers between devices with their start and end apart: 7 -> 0, of which waited for: 5 -> 0; matrix products, arithmetic and copies ran while one was open for 11% -> 0% of each run, Pallas kernels for 0% -> 0%
where the time goes in v2:
time: 105 us
  Pallas kernels  98 us (93%)
  local copies, waits for them, and re-layouts  5.37 us (5%)
  between operations  1.41 us (1%)
    pallas_call x1, Pallas kernels, collect(): pl.pallas_call(collect_kernel, out_shape=(jax.ShapeDtypeStruct((FRAG, SLA...  43.9 us
    pallas_call x1, Pallas kernels, spread(): pl.pallas_call(spread_kernel, out_shape=(jax.ShapeDtypeStruct((FRAG, SLAB...  42.2 us
    pallas_call x1, Pallas kernels, pair_terms(): pl.pallas_call(pair_kernel, out_shape=jax.ShapeDtypeStruct((TURNS, 2, ROW...  9.01 us
    unnamed x19, local copies, waits for them, and re-layouts  4.09 us

profile of v2, /device:TPU:1, one launch (start us, length us, event | category | flops | bytes accessed | tf_op | source)
XLA Modules:
  0.0 104.8 jit_solution(354264754344922111)
XLA Ops:
  0.6 0.0 copy-start.6
  0.6 0.0 copy-start.7
  0.7 0.0 copy-start.4
  0.7 0.0 copy-start.3
  0.7 0.0 copy-start.8
  0.7 1.3 %reshape.13.mine = f32[2,4,216,128]{3,2,1,0:T(8,128)S(1)} reshape(f32[2,48,2304]{2,1,0:T(8,128)} %param.11) | data formatting | bytes 1769472 | tf_op jit(solution)/shard_map/reshape | solution.py:511
  2.0 0.0 copy-done.6
  2.0 0.0 copy-done.7
  2.0 0.0 copy-done.4
  2.0 42.2 %spread.1 = (f32[8,216,128]{2,1,0:T(8,128)S(1)}, f32[2,2,864,128]{3,2,1,0:T(8,128)S(1)}) custom-call(f32[2,4,216,128]{3,2,1,0:T(8,128)S(1)} %reshape.13.mine, s32[8]{0:T(128)S(1)} %copy-done.6, s32[8]{0:T(128)S(1)} %copy-done.7, s32[8]{0:T(128)S(1)} %copy-done.4), custom_call_target="tpu_custom_call" | custom-call | tf_op jit(solution)/shard_map/spread/pallas_call | solution.py:354
  44.2 0.0 copy-start.1
  44.2 1.2 %copy-done.1 = f32[2,2,864,128]{3,2,1,0:T(8,128)} copy-done((f32[2,2,864,128]{3,2,1,0:T(8,128)}, f32[2,2,864,128]{3,2,1,0:T(8,128)S(1)}, u32[]{:S(2)}) %copy-start.1) | copy-done | bytes 1769496
  45.4 0.0 copy-done.3
  45.4 1.0 mode_table.1.modes_ref
  46.5 0.0 copy-start.2
  46.5 0.7 copy-done.2
  47.2 0.0 copy-done.8
  47.2 0.7 copy.13.anchors
  47.9 9.0 %pair_terms.1 = f32[2,2,864,128]{3,2,1,0:T(8,128)} custom-call(f32[2,2,864,128]{3,2,1,0:T(8,128)} %copy-done.1, f32[152,384]{1,0:T(8,128)} %copy-done.2, bf16[304,576]{1,0:T(8,128)(2,1)} %constant.8.clone.left_ref, bf16[288,608]{1,0:T(8,128)(2,1)} %constant.9.clone.inverse_ref, bf16[768,768]{1,0:T(8,128)(2,1)} %constant.10.clone.right_ref, ...), custom_call_target="tpu_custom_call" | custom-call | tf_op jit(solution)/shard_map/pair_terms/pallas_call | solution.py:213
  57.5 0.0 copy-done.5
  57.5 0.0 copy-start
  57.6 1.5 %copy-done = f32[2,2,864,128]{3,2,1,0:T(8,128)S(1)} copy-done((f32[2,2,864,128]{3,2,1,0:T(8,128)S(1)}, f32[2,2,864,128]{3,2,1,0:T(8,128)}, u32[]{:S(2)}) %copy-start) | copy-done | bytes 1769496
  59.0 43.9 %collect.1 = (f32[8,216,128]{2,1,0:T(8,128)S(1)}, f32[8,128]{1,0:T(8,128)S(1)}) custom-call(f32[2,2,4,216,128]{4,3,2,1,0:T(8,128)S(1)} %bitcast.4, f32[8,216,128]{2,1,0:T(8,128)S(1)} %get-tuple-element.8.phi_ref, s32[1]{0:T(128)S(6)} %copy.14.count, s32[8]{0:T(128)S(1)} %copy-done.6, s32[8]{0:T(128)S(1)} %copy-done.7, s32[8]{0:T(128)S(1)} %copy-done.5), custom_call_target="tpu_custom_call" | custom-call | tf_op jit(solution)/shard_map/collect/pallas_call | solution.py:463
  102.9 1.9 %projected.1 = (f32[96,2304]{1,0:T(8,128)}, f32[1,8,8]{2,1,0:T(8,128)}) custom-call(f32[8,216,128]{2,1,0:T(8,128)S(1)} %get-tuple-element.8.phi_ref, f32[8,216,128]{2,1,0:T(8,128)S(1)} %get-tuple-element.10.action_ref, f32[8,128]{1,0:T(8,128)S(1)} %get-tuple-element.11.total_ref), custom_call_target="tpu_custom_call" | custom-call | tf_op jit(solution)/shard_map/projected/pallas_call | solution.py:497
  (1 shorter events, 0.0 us)
Async XLA Ops:
  0.6 1.3 %copy-start.6 = (s32[8]{0:T(128)S(1)}, s32[8]{0:T(128)}, u32[]{:S(2)}) copy-start(s32[8]{0:T(128)} %first.3) | copy-start | bytes 100
  0.6 1.3 %copy-start.7 = (s32[8]{0:T(128)S(1)}, s32[8]{0:T(128)}, u32[]{:S(2)}) copy-start(s32[8]{0:T(128)} %second.3) | copy-start | bytes 100
  0.7 1.3 %copy-start.4 = (s32[8]{0:T(128)S(1)}, s32[8]{0:T(128)}, u32[]{:S(2)}) copy-start(s32[8]{0:T(128)} %reach.3) | copy-start | bytes 100
  0.7 44.8 %copy-start.3 = (f32[48,2304]{1,0:T(8,128)S(1)}, f32[48,2304]{1,0:T(8,128)}, u32[]{:S(2)}) copy-start(f32[48,2304]{1,0:T(8,128)} %kernel_ref.1) | copy-start | bytes 1327108
  0.7 46.5 %copy-start.8 = (s32[64,3]{0,1:T(4,128)S(1)}, s32[64,3]{0,1:T(4,128)}, u32[]{:S(2)}) copy-start(s32[64,3]{0,1:T(4,128)} %param.13) | copy-start | bytes 2308
  44.2 1.2 %copy-start.1 = (f32[2,2,864,128]{3,2,1,0:T(8,128)}, f32[2,2,864,128]{3,2,1,0:T(8,128)S(1)}, u32[]{:S(2)}) copy-start(f32[2,2,864,128]{3,2,1,0:T(8,128)S(1)} %get-tuple-element.9.pairs_ref) | copy-start | bytes 5308420
  46.5 0.7 copy-start.2
  47.9 9.7 %copy-start.5 = (s32[8]{0:T(128)S(1)}, s32[8]{0:T(128)}, u32[]{:S(2)}) copy-start(s32[8]{0:T(128)} %reach.3) | copy-start | bytes 100
  57.5 1.5 %copy-start = (f32[2,2,864,128]{3,2,1,0:T(8,128)S(1)}, f32[2,2,864,128]{3,2,1,0:T(8,128)}, u32[]{:S(2)}) copy-start(f32[2,2,864,128]{3,2,1,0:T(8,128)} %pair_terms.1) | copy-start | bytes 5308420

commit v3 on v2

--- a/solution.py
+++ b/solution.py
@@ -22,7 +22,7 @@
 CH = 152
 PADX = 16
 PADT = 8
-CHUNKS = 3
+CHUNKS = 9
 CHUNK = SLAB // CHUNKS
 
 
@@ -95,7 +95,7 @@
         in_specs=[vmem],
         out_specs=vmem,
         scratch_shapes=[pltpu.VMEM((288, 384), jnp.float32), pltpu.VMEM((288, 384), jnp.float32)],
-        compiler_params=pltpu.CompilerParams(vmem_limit_bytes=40 << 20),
+        compiler_params=pltpu.CompilerParams(vmem_limit_bytes=6 << 20),
         name="mode_table",
     )(kernel)
 
@@ -136,7 +136,7 @@
 
     def offset_of(turn):
         partner = lax.rem(frag + reach_ref[member + GRP * turn], lax.axis_size("orb"))
-        return [anchors[partner, k] - anchors[frag, k] for k in range(3)]
+        return [anchors[k, partner] - anchors[k, frag] for k in range(3)]
 
     padded[...] = jnp.zeros_like(padded)
 
@@ -227,7 +227,7 @@
             pltpu.VMEM((1152, 768), jnp.bfloat16),
             pltpu.VMEM((2, CH, 384), jnp.float32),
         ],
-        compiler_params=pltpu.CompilerParams(vmem_limit_bytes=56 << 20),
+        compiler_params=pltpu.CompilerParams(vmem_limit_bytes=24 << 20),
         name="pair_terms",
     )(pairs, modes, jnp.asarray(left), jnp.asarray(inverse), jnp.asarray(right), jnp.asarray(twiddle), anchors, reach)
 
@@ -361,7 +361,7 @@
         + [pltpu.VMEM((GRP, TURNS, CHUNK, 128), jnp.float32)] * (2 * CHUNKS)
         + [dma((CHUNKS, GRP)), dma((CHUNKS, GRP)), dma((CHUNKS,)), dma((CHUNKS,)), dma((CHUNKS,)),
            dma((CHUNKS,)), dma((CHUNKS,)), dma((2, CHUNKS, GRP)), dma((2, CHUNKS, GRP))],
-        compiler_params=pltpu.CompilerParams(collective_id=0, has_side_effects=True, vmem_limit_bytes=40 << 20),
+        compiler_params=pltpu.CompilerParams(collective_id=0, has_side_effects=True, vmem_limit_bytes=14 << 20),
         name="spread",
     )(mine, first, second, reach)
 
@@ -473,7 +473,7 @@
            pltpu.VMEM((GRP, FRAG, 128), jnp.float32),
            dma((CHUNKS, GRP)), dma((CHUNKS, GRP)), dma((CHUNKS,)), dma((CHUNKS,)), dma((CHUNKS,)), dma((CHUNKS,)),
            dma((GRP,)), dma((GRP,))],
-        compiler_params=pltpu.CompilerParams(collective_id=1, has_side_effects=True, vmem_limit_bytes=40 << 20),
+        compiler_params=pltpu.CompilerParams(collective_id=1, has_side_effects=True, vmem_limit_bytes=14 << 20),
         name="collect",
     )(terms, phi, count, first, second, reach)
 
@@ -501,7 +501,7 @@
         in_specs=[vmem] * 3,
         out_specs=(vmem, vmem),
         scratch_shapes=[pltpu.VMEM((FRAG * SLAB, 128), jnp.float32)],
-        compiler_params=pltpu.CompilerParams(vmem_limit_bytes=40 << 20),
+        compiler_params=pltpu.CompilerParams(vmem_limit_bytes=8 << 20),
         name="projected",
     )(phi, action, total)
 
@@ -510,7 +510,7 @@
     modes = mode_table(kernel)
     mine = orbitals.reshape(2, GRP, SLAB, 128)
     phi, pairs = spread(mine, pair_first, pair_second, pair_reach)
-    terms = pair_terms(pairs, modes, anchors, pair_reach).reshape(TURNS, 2, GRP, SLAB, 128)
+    terms = pair_terms(pairs, modes, anchors.T, pair_reach).reshape(TURNS, 2, GRP, SLAB, 128)
     action, total = collect(terms, phi, pair_count, pair_first, pair_second, pair_reach)
     gradient, lagrange = projected(phi, action, total)
     return gradient.reshape(12, FRAG, B * B).transpose(1, 0, 2), lagrange

time: 105 us -> 95.4 us (0.909)
  Pallas kernels: 98 us -> 89.1 us
    pallas_call x1, Pallas kernels: 43.9 us -> 37.1 us  [collect(): pl.pallas_call(collect_kernel, out_shape=(jax.ShapeDtypeStruct((FRAG, SLA...]
    pallas_call x1, Pallas kernels: 9.01 us -> 6.26 us  [pair_terms(): pl.pallas_call(pair_kernel, out_shape=jax.ShapeDtypeStruct((TURNS, 2, ROW...]
    unnamed x19 -> x24, local copies, waits for them, and re-layouts: 4.09 us -> 3.33 us
where the time goes in v3:
time: 95.4 us; the launch traced here: 95.2 us
  Pallas kernels  89.1 us (93%)
  local copies, waits for them, and re-layouts  4.71 us (5%)
  between operations  1.43 us (1%)
    pallas_call x1, Pallas kernels, spread(): pl.pallas_call(spread_kernel, out_shape=(jax.ShapeDtypeStruct((FRAG, SLAB...  42.8 us
    pallas_call x1, Pallas kernels, collect(): pl.pallas_call(collect_kernel, out_shape=(jax.ShapeDtypeStruct((FRAG, SLA...  37.1 us
    pallas_call x1, Pallas kernels, pair_terms(): pl.pallas_call(pair_kernel, out_shape=jax.ShapeDtypeStruct((TURNS, 2, ROW...  6.26 us
    unnamed x24, local copies, waits for them, and re-layouts  3.33 us
    pallas_call x1, Pallas kernels, projected(): pl.pallas_call(project_kernel, out_shape=(jax.ShapeDtypeStruct((12 * FRAG...  1.93 us

profile of v3, /device:TPU:1, one launch (start us, length us, event | category | flops | bytes accessed | tf_op | source)
XLA Modules:
  0.0 95.2 jit_solution(11441115717509079021)
XLA Ops:
  0.6 0.0 copy-start
  0.6 0.0 copy-start.4
  0.7 0.0 copy-start.2
  0.7 0.0 copy-start.3
  0.7 0.0 copy-start.1
  0.7 1.4 %reshape.13.mine = f32[2,4,216,128]{3,2,1,0:T(8,128)S(1)} reshape(f32[2,48,2304]{2,1,0:T(8,128)} %param.11) | data formatting | bytes 1769472 | tf_op jit(solution)/shard_map/reshape | solution.py:511
  2.1 0.0 copy-start.5
  2.1 0.6 copy-done.5
  2.7 0.7 copy-done.8
  3.4 0.7 copy-done.10
  4.0 42.8 %spread.1 = (f32[8,216,128]{2,1,0:T(8,128)S(1)}, f32[2,2,864,128]{3,2,1,0:T(8,128)S(1)}) custom-call(f32[2,4,216,128]{3,2,1,0:T(8,128)S(1)} %reshape.13.mine, s32[8]{0:T(128)S(1)} %copy-done.8, s32[8]{0:T(128)S(1)} %copy-done.10, s32[8]{0:T(128)S(1)} %copy-done.5), custom_call_target="tpu_custom_call" | custom-call | tf_op jit(solution)/shard_map/spread/pallas_call | solution.py:354
  46.9 0.0 copy-done.1
  46.9 1.0 %mode_table.1.modes_ref = f32[152,384]{1,0:T(8,128)S(1)} custom-call(f32[48,2304]{1,0:T(8,128)S(1)} %copy-done.1), custom_call_target="tpu_custom_call" | custom-call | tf_op jit(solution)/shard_map/mode_table/pallas_call | solution.py:92
  47.9 0.0 copy-done
  47.9 0.0 copy-done.4
  47.9 0.0 copy-done.2
  47.9 0.0 copy-done.3
  47.9 0.0 copy-start.6
  48.0 0.6 copy-done.6
  48.6 0.7 copy-done.7
  49.3 6.3 %pair_terms.1 = f32[2,2,864,128]{3,2,1,0:T(8,128)S(1)} custom-call(f32[2,2,864,128]{3,2,1,0:T(8,128)S(1)} %get-tuple-element.9.pairs_ref, f32[152,384]{1,0:T(8,128)S(1)} %mode_table.1.modes_ref, bf16[304,576]{1,0:T(8,128)(2,1)S(1)} %copy-done.2, bf16[288,608]{1,0:T(8,128)(2,1)S(1)} %copy-done.3, bf16[768,768]{1,0:T(8,128)(2,1)S(1)} %copy-done, ...), custom_call_target="tpu_custom_call" | custom-call | tf_op jit(solution)/shard_map/pair_terms/pallas_call | solution.py:213
  56.2 0.0 copy-done.9
  56.2 37.1 %collect.1 = (f32[8,216,128]{2,1,0:T(8,128)S(1)}, f32[8,128]{1,0:T(8,128)S(1)}) custom-call(f32[2,2,4,216,128]{4,3,2,1,0:T(8,128)S(1)} %bitcast.5, f32[8,216,128]{2,1,0:T(8,128)S(1)} %get-tuple-element.8.phi_ref, s32[1]{0:T(128)S(6)} %copy.13.count, s32[8]{0:T(128)S(1)} %copy-done.9, s32[8]{0:T(128)S(1)} %copy-done.11, s32[8]{0:T(128)S(1)} %copy-done.6), custom_call_target="tpu_custom_call" | custom-call | tf_op jit(solution)/shard_map/collect/pallas_call | solution.py:463
  93.3 1.9 %projected.1 = (f32[96,2304]{1,0:T(8,128)}, f32[1,8,8]{2,1,0:T(8,128)}) custom-call(f32[8,216,128]{2,1,0:T(8,128)S(1)} %get-tuple-element.8.phi_ref, f32[8,216,128]{2,1,0:T(8,128)S(1)} %get-tuple-element.10.action_ref, f32[8,128]{1,0:T(8,128)S(1)} %get-tuple-element.11.total_ref), custom_call_target="tpu_custom_call" | custom-call | tf_op jit(solution)/shard_map/projected/pallas_call | solution.py:497
  (6 shorter events, 0.0 us)
Async XLA Ops:
  0.6 47.3 %copy-start = (bf16[768,768]{1,0:T(8,128)(2,1)S(1)}, bf16[768,768]{1,0:T(8,128)(2,1)}, u32[]{:S(2)}) copy-start(bf16[768,768]{1,0:T(8,128)(2,1)} %constant.10.clone.right_ref) | copy-start | bytes 3538948
  0.6 47.3 %copy-start.4 = (f32[2,6,384]{2,1,0:T(8,128)S(1)}, f32[2,6,384]{2,1,0:T(8,128)}, u32[]{:S(2)}) copy-start(f32[2,6,384]{2,1,0:T(8,128)} %constant.11.clone.twiddle_ref) | copy-start | bytes 55300
  0.7 47.3 %copy-start.2 = (bf16[304,576]{1,0:T(8,128)(2,1)S(1)}, bf16[304,576]{1,0:T(8,128)(2,1)}, u32[]{:S(2)}) copy-start(bf16[304,576]{1,0:T(8,128)(2,1)} %constant.8.clone.left_ref) | copy-start | bytes 1050628
  0.7 47.3 %copy-start.3 = (bf16[288,608]{1,0:T(8,128)(2,1)S(1)}, bf16[288,608]{1,0:T(8,128)(2,1)}, u32[]{:S(2)}) copy-start(bf16[288,608]{1,0:T(8,128)(2,1)} %constant.9.clone.inverse_ref) | copy-start | bytes 1050628
  0.7 46.2 %copy-start.1 = (f32[48,2304]{1,0:T(8,128)S(1)}, f32[48,2304]{1,0:T(8,128)}, u32[]{:S(2)}) copy-start(f32[48,2304]{1,0:T(8,128)} %kernel_ref.1) | copy-start | bytes 1327108
  2.1 0.7 copy-start.5
  2.7 0.7 copy-start.8
  3.4 0.7 copy-start.10
  47.9 0.7 copy-start.6
  48.6 0.7 copy-start.7
  49.3 6.9 %copy-start.9 = (s32[8]{0:T(128)S(1)}, s32[8]{0:T(128)}, u32[]{:S(2)}) copy-start(s32[8]{0:T(128)} %first.3) | copy-start | bytes 100
  49.3 6.9 %copy-start.11 = (s32[8]{0:T(128)S(1)}, s32[8]{0:T(128)}, u32[]{:S(2)}) copy-start(s32[8]{0:T(128)} %second.3) | copy-start | bytes 100

commit v4 on v3

v4 whole, which is shorter than its diff:
```python
import functools
import math

import jax
import jax.numpy as jnp
import ml_dtypes
import numpy as np
from jax import lax
from jax.experimental import pallas as pl
from jax.experimental.pallas import tpu as pltpu
from jax.sharding import PartitionSpec as P

MESH = pl.DeviceIdType.MESH
B = 48
FRAG = 8
GRP = 4
TURNS = 2
TILES = 18
SLAB = 216
ROWS = 864
HALF = 25
CH = 152
PADX = 16
PADT = 8
CHUNKS = 9
CHUNK = SLAB // CHUNKS


def split(a):
    a = a.astype(np.float32)
    head = a.astype(ml_dtypes.bfloat16)
    tail = (a - head.astype(np.float32)).astype(ml_dtypes.bfloat16)
    return head, tail


@functools.lru_cache(None)
def tables():
    c, kx = np.meshgrid(np.arange(6), np.arange(HALF), indexing="ij")
    c, kx = c.reshape(-1, 1), kx.reshape(-1, 1)
    a, x = np.meshgrid(np.arange(6), np.arange(B), indexing="ij")
    a, x = a.reshape(1, -1), x.reshape(1, -1)
    theta = 2 * np.pi * ((8 * c * a + kx * x) % 48) / 48
    left = np.zeros((2 * CH, 288))
    left[:150] = np.cos(theta)
    left[CH:CH + 150] = -np.sin(theta)
    left = np.concatenate(split(left), axis=1)
    inverse = np.concatenate([left[:, :288].T, left[:, 288:].T], axis=1)
    b, z = np.meshgrid(np.arange(8), np.arange(B), indexing="ij")
    b, z = b.reshape(-1), z.reshape(-1)
    phi = 2 * np.pi * ((6 * np.outer(b, b) + np.outer(z, z)) % 48) / 48
    right = np.concatenate(split(np.concatenate([np.cos(phi), -np.sin(phi)], axis=1)), axis=0)
    turn = 2 * np.pi * ((np.arange(6)[:, None] * b[None, :]) % 48) / 48
    twiddle = np.stack([np.cos(turn), -np.sin(turn)]).astype(np.float32)
    return left, inverse, right, twiddle


def halves(value):
    head = value.astype(jnp.bfloat16)
    return head, (value - head.astype(jnp.float32)).astype(jnp.bfloat16)


def dot(a, b):
    return jnp.dot(a, b, preferred_element_type=jnp.float32)


def modes_of(kernel_ref, modes_ref, picked, mirrored):
    for c in range(6):
        for e in range(8):
            picked[48 * c:48 * c + 48, 48 * e:48 * e + 48] = kernel_ref[:, 48 * (c + 6 * e):48 * (c + 6 * e) + 48]
    lane = lax.broadcasted_iota(jnp.int32, (1, 384), 1)
    e, kz = lane // B, lane % B
    row = lax.broadcasted_iota(jnp.int32, (384, 384), 0)
    for shift, rows in ((0, slice(0, 48)), (1, slice(48, 288))):
        source = (16 - e - shift) % 8 * B + (B - kz) % B
        permute = jnp.where(row == source, 1.0, 0.0).astype(jnp.bfloat16)
        head, tail = halves(picked[rows, :])
        mirrored[rows, :] = dot(head, permute) + dot(tail, permute)
    out = lax.broadcasted_iota(jnp.int32, (32, B), 0)
    permute = jnp.where(lax.broadcasted_iota(jnp.int32, (32, B), 1) == (B - out) % B, 1.0, 0.0).astype(jnp.bfloat16)
    kx = lax.broadcasted_iota(jnp.int32, (32, 384), 0)
    weight = jnp.where((kx == 0) | (kx == HALF - 1), 0.5 / B**3, 1.0 / B**3)
    modes_ref[144:CH, :] = jnp.zeros((8, 384), jnp.float32)
    for c in range(6):
        other = (6 - c) % 6
        head, tail = halves(mirrored[48 * other:48 * other + 48, :])
        even = (picked[48 * c:48 * c + 32, :] + dot(permute, head) + dot(permute, tail)) * weight
        modes_ref[HALF * c:HALF * c + HALF, :] = even[:HALF]


def shifted(source, offset, emit):
    d0, d1, d2 = offset
    flat = 48 * d1 + d2 + 1024
    tile = lax.shift_right_logical(flat, 7) - 8
    lane_by = lax.bitwise_and(flat, 127)
    lane = lax.broadcasted_iota(jnp.int32, (B, 128), 1)
    late = lane >= lane_by
    insides = []
    for k in range(3):
        z = lax.rem(lane + 128 * k, B) - d2
        insides.append((z >= 0) & (z < B))
    before = None
    for t in range(-1, TILES):
        block = source[t - tile + PADT, pl.ds(PADX - d0, B), :]
        block = pltpu.roll(block, lane_by, 1)
        if t >= 0:
            emit(t, jnp.where(insides[t % 3], jnp.where(late, block, before), 0.0))
        before = block


def stack_tables(left_ref, inverse_ref, right_ref, twiddle_ref, left, inverse, right, twiddle):
    left[:, 0:288] = left_ref[:, 0:288]
    left[:, 288:864] = left_ref[...]
    inverse[:, 0:304] = inverse_ref[:, 0:304]
    inverse[:, 304:912] = inverse_ref[...]
    right[0:384, :] = right_ref[0:384, :]
    right[384:1152, :] = right_ref[...]
    for c in range(6):
        rows = slice(HALF * c, HALF * c + HALF + 2 * (c == 5))
        for part in range(2):
            twiddle[part, rows, :] = jnp.broadcast_to(twiddle_ref[part, c:c + 1, :], (rows.stop - rows.start, 384))


def block_of(t):
    return slice(48 * (t // 3), 48 * (t // 3) + 48), slice(128 * (t % 3), 128 * (t % 3) + 128)


def potentials(pairs, offsets, modes, left, inverse, right, twiddle, padded, moved, stack, wide, spec, volume):
    for turn in range(TURNS):
        for t in range(TILES):
            padded[t + PADT, pl.ds(PADX, B), :] = pairs[turn, 1, pl.ds(t, B, stride=TILES), :]

        def emit(t, block):
            moved[turn, t] = block
            density = pairs[turn, 0, pl.ds(t, B, stride=TILES), :] * block
            head, tail = halves(density)
            rows, lanes = block_of(t)
            lanes = slice(384 * turn + lanes.start, 384 * turn + lanes.stop)
            stack[rows.start:rows.stop, lanes] = head
            stack[288 + rows.start:288 + rows.stop, lanes] = tail
            stack[576 + rows.start:576 + rows.stop, lanes] = head

        shifted(padded, offsets[turn], emit)

    volume[0:2 * CH, :] = dot(left[...], stack[0:864, :])
    tr, ti = twiddle[0], twiddle[1]

    def put(row, value):
        head, tail = halves(value)
        wide[row:row + CH, 0:384] = head
        wide[row:row + CH, 384:768] = tail
        wide[row:row + CH, 768:1152] = head

    for turn in range(TURNS):
        re = volume[0:CH, 384 * turn:384 * turn + 384]
        im = volume[CH:2 * CH, 384 * turn:384 * turn + 384]
        put(2 * CH * turn, re * tr - im * ti)
        put(2 * CH * turn + CH, re * ti + im * tr)
    spec[...] = dot(wide[...], right[...])
    table = modes[...]
    for turn in range(TURNS):
        row = 2 * CH * turn
        re = spec[row:row + CH, 0:384] - spec[row + CH:row + 2 * CH, 384:768]
        im = spec[row:row + CH, 384:768] + spec[row + CH:row + 2 * CH, 0:384]
        put(row, re * table)
        put(row + CH, im * table)
    spec[...] = dot(wide[...], right[...])
    for turn in range(TURNS):
        row = 2 * CH * turn
        re = spec[row:row + CH, 0:384] + spec[row + CH:row + 2 * CH, 384:768]
        im = spec[row + CH:row + 2 * CH, 0:384] - spec[row:row + CH, 384:768]
        lanes = slice(384 * turn, 384 * turn + 384)
        for part, value in enumerate((re * tr + im * ti, im * tr - re * ti)):
            head, tail = halves(value)
            stack[CH * part:CH * part + CH, lanes] = head
            stack[304 + CH * part:304 + CH * part + CH, lanes] = tail
            stack[608 + CH * part:608 + CH * part + CH, lanes] = head
    volume[0:288, :] = dot(inverse[...], stack[...])


def terms_of(turn, pairs, offset, volume, moved, padded, terms):
    for t in range(TILES):
        rows, lanes = block_of(t)
        potential = volume[rows, 384 * turn + lanes.start:384 * turn + lanes.stop]
        terms[turn, 0, pl.ds(t, B, stride=TILES), :] = potential * moved[turn, t]
        padded[t + PADT, pl.ds(PADX, B), :] = potential * pairs[turn, 0, pl.ds(t, B, stride=TILES), :]

    def emit(t, block):
        terms[turn, 1, pl.ds(t, B, stride=TILES), :] = block

    shifted(padded, [-d for d in offset], emit)


def sibling(orb):
    return orb + 1 - 2 * lax.rem(orb, 2)


def exchange_kernel(orbitals, kernel, left_hbm, inverse_hbm, right_hbm, twiddle_hbm, anchors_hbm, count_hbm, first_hbm,
                    second_hbm, reach_hbm, phi_ref, action_ref, total_ref, *scratch):
    scratch = list(scratch)

    def take(n):
        taken, scratch[:] = scratch[:n], scratch[n:]
        return taken

    near = take(3 * CHUNKS)
    out = take(2 * CHUNKS)
    landed, aside, beside, onward, behind = (take(CHUNKS) for _ in range(5))
    native, kernel_ref, left_ref, inverse_ref, right_ref, twiddle_ref = take(6)
    anchors, count, first, second, reach = take(5)
    mine, pairs, terms, modes, picked, mirrored, left, inverse, right, twiddle = take(10)
    padded, moved, stack, wide, spec, volume = take(6)
    products, block, blocks = take(3)
    (load_sem, send_slab, recv_slab, own_sem, send_ahead, recv_ahead, send_side, recv_side, send_pick, recv_pick,
     send_term, recv_term, send_back, recv_back, send_on, recv_on, send_sum, recv_sum) = scratch
    orb, me = lax.axis_index("orb"), lax.axis_index("grp")
    orbs = lax.axis_size("orb")
    even = lax.rem(orb, 2) == 0
    is_even = jnp.where(even, 1.0, 0.0)
    sources = (orbitals, first_hbm, second_hbm, reach_hbm, kernel, left_hbm, inverse_hbm, right_hbm, twiddle_hbm,
               anchors_hbm, count_hbm)
    places = (native, first, second, reach, kernel_ref, left_ref, inverse_ref, right_ref, twiddle_ref, anchors, count)
    loads = [pltpu.make_async_copy(s, p, load_sem.at[i]) for i, (s, p) in enumerate(zip(sources, places))]
    for load in loads:
        load.start()
    barrier = pltpu.get_barrier_semaphore()
    for step in range(1, GRP):
        pl.semaphore_signal(barrier, inc=1, device_id={"grp": lax.rem(me + step, GRP)}, device_id_type=MESH)
    for other in (sibling(orb), lax.rem(orb + 2, orbs), lax.rem(orb + orbs - 2, orbs)):
        pl.semaphore_signal(barrier, inc=1, device_id={"orb": other}, device_id_type=MESH)
    loads[0].wait()
    for j in range(2):
        for t in range(TILES):
            mine[j, pl.ds(t, B, stride=TILES), :] = native[j, :, 128 * t:128 * t + 128]
    pl.semaphore_wait(barrier, GRP - 1 + 3)

    def rows(c):
        return pl.ds(CHUNK * c, CHUNK)

    def peers():
        return [(step, lax.rem(me + step, GRP)) for step in (2, 1, 3)]

    def at_slab(member, c):
        return pl.ds(pl.multiple_of(SLAB * member + CHUNK * c, 8), CHUNK)

    slabs, owns = [], []
    for c in range(CHUNKS):
        slabs.append([pltpu.make_async_remote_copy(
            src_ref=mine.at[:, at_slab(other, c)], dst_ref=near[3 * c].at[pl.ds(2 * me, 2)],
            send_sem=send_slab.at[c, step], recv_sem=recv_slab.at[c, step],
            device_id={"grp": other}, device_id_type=MESH) for step, other in peers()])
        owns.append(pltpu.make_async_copy(mine.at[:, at_slab(me, c)], near[3 * c].at[pl.ds(2 * me, 2)], own_sem.at[c]))
        owns[c].start()
        for copy in slabs[c]:
            copy.start()

    ahead = [pltpu.make_async_remote_copy(
        src_ref=near[3 * c], dst_ref=near[3 * c + 2], send_sem=send_ahead.at[c], recv_sem=recv_ahead.at[c],
        device_id={"orb": lax.rem(orb + orbs - 2, orbs)}, device_id_type=MESH) for c in range(CHUNKS)]
    side = [[pltpu.make_async_remote_copy(
        src_ref=near[3 * c + which], dst_ref=near[3 * c + 1], send_sem=send_side.at[c], recv_sem=recv_side.at[c],
        device_id={"orb": sibling(orb)}, device_id_type=MESH) for which in (2, 0)] for c in range(CHUNKS)]
    picks = [[[pltpu.make_async_remote_copy(
        src_ref=out[2 * c + which].at[other], dst_ref=pairs.at[:, which, at_slab(me, c)],
        send_sem=send_pick.at[which, c, step], recv_sem=recv_pick.at[which, c, step],
        device_id={"grp": other}, device_id_type=MESH) for step, other in peers()]
        for c in range(CHUNKS)] for which in range(2)]

    def choose(which, c):
        for slot in range(GRP * TURNS):
            if which == 0:
                value = near[3 * c][first[slot]]
            else:
                value = near[3 * c][second[slot]]
                value = jnp.where(reach[slot] == 1, near[3 * c + 1][second[slot]], value)
                value = jnp.where(reach[slot] == 2, near[3 * c + 2][second[slot]], value)
            out[2 * c + which][slot % GRP, slot // GRP] = value
        for copy in picks[which][c]:
            copy.start()
        pairs[:, which, at_slab(me, c), :] = out[2 * c + which][me]

    for load in loads[1:4]:
        load.wait()
    for c in range(CHUNKS):
        owns[c].wait()
        for copy in slabs[c]:
            copy.wait_recv()
        ahead[c].start()

        @pl.when(jnp.logical_not(even))
        def _():
            side[c][1].start()

        choose(0, c)
        phi_ref[:, CHUNK * c:CHUNK * c + CHUNK, :] = near[3 * c][...]
        if c == 0:
            for load in loads[4:]:
                load.wait()
            stack_tables(left_ref, inverse_ref, right_ref, twiddle_ref, left, inverse, right, twiddle)
        if c == 1:
            modes_of(kernel_ref, modes, picked, mirrored)
        if c == 2:
            padded[...] = jnp.zeros_like(padded)
    for c in range(CHUNKS + 1):
        if c < CHUNKS:
            ahead[c].wait_recv()

            @pl.when(even)
            def _():
                side[c][0].start()

        if c > 0:
            side[c - 1][0].wait_recv()
            choose(1, c - 1)
    for c in range(CHUNKS):
        for which in range(2):
            for copy in picks[which][c]:
                copy.wait_recv()

    offsets = []
    for turn in range(TURNS):
        far = reach[me + GRP * turn]
        offsets.append([anchors[k, lax.rem(orb + far, orbs)] - anchors[k, orb] for k in range(3)])
    potentials(pairs, offsets, modes, left, inverse, right, twiddle, padded, moved, stack, wide, spec, volume)

    sends = [[[pltpu.make_async_remote_copy(
        src_ref=terms.at[turn, :, at_slab(other, c)], dst_ref=landed[c].at[me, turn],
        send_sem=send_term.at[turn, c, step], recv_sem=recv_term.at[turn, c, step],
        device_id={"grp": other}, device_id_type=MESH) for step, other in peers()]
        for c in range(CHUNKS)] for turn in range(TURNS)]
    early = 2
    for turn in range(TURNS):
        terms_of(turn, pairs, offsets[turn], volume, moved, padded, terms)
        for c in range(CHUNKS):
            for other_turn in range(TURNS):
                if turn == (0 if other_turn == 0 and c < early else 1):
                    for copy in sends[other_turn][c]:
                        copy.start()
    back = [pltpu.make_async_remote_copy(
        src_ref=aside[c], dst_ref=beside[c], send_sem=send_back.at[c], recv_sem=recv_back.at[c],
        device_id={"orb": sibling(orb)}, device_id_type=MESH) for c in range(CHUNKS)]
    on = [pltpu.make_async_remote_copy(
        src_ref=onward[c], dst_ref=behind[c], send_sem=send_on.at[c], recv_sem=recv_on.at[c],
        device_id={"orb": lax.rem(orb + 2, orbs)}, device_id_type=MESH) for c in range(CHUNKS)]
    live = [jnp.where(slot < count[0], 1.0, 0.0) for slot in range(GRP * TURNS)]

    def summed(c, a, which, far):
        value = jnp.zeros((CHUNK, 128), jnp.float32)
        for slot in range(GRP * TURNS):
            term = landed[c][slot % GRP, slot // GRP, which]
            if which == 0:
                weight = jnp.where(first[slot] == a, live[slot], 0.0)
            else:
                weight = jnp.where((second[slot] == a) & (reach[slot] == far), live[slot], 0.0)
            value = value + weight * term
        return value

    for c in range(CHUNKS):
        landed[c][me] = terms[:, :, at_slab(me, c), :]
    for c in range(CHUNKS):
        for turn in range(TURNS):
            for copy in sends[turn][c]:
                copy.wait_recv()
        for a in range(FRAG):
            aside[c][a] = summed(c, a, 1, 1)
        back[c].start()
        for a in range(FRAG):
            onward[c][a] = summed(c, a, 1, 2)
            action_ref[a, CHUNK * c:CHUNK * c + CHUNK, :] = summed(c, a, 0, 0) + summed(c, a, 1, 0)
        back[c].wait_recv()
        for a in range(FRAG):
            onward[c][a] = onward[c][a] + is_even * beside[c][a]
        on[c].start()
    products[...] = jnp.zeros_like(products)
    for c in range(CHUNKS):
        on[c].wait_recv()
        for b in range(FRAG):
            value = action_ref[b, CHUNK * c:CHUNK * c + CHUNK, :] + behind[c][b] + (1.0 - is_even) * beside[c][b]
            action_ref[b, CHUNK * c:CHUNK * c + CHUNK, :] = value
            for a in range(FRAG):
                part = jnp.sum((phi_ref[a, CHUNK * c:CHUNK * c + CHUNK, :] * value).reshape(CHUNK // 8, 8, 128), axis=0)
                products[b, a] = products[b, a] + part
    lane = lax.broadcasted_iota(jnp.int32, (FRAG, 128), 1)
    total = jnp.zeros((FRAG, 128), jnp.float32)
    for b in range(FRAG):
        part = jnp.sum(jnp.sum(products[b], axis=1), axis=1, keepdims=True)
        total = total + jnp.where(lane == b, part, 0.0)
    block[...] = total
    sums = []
    for step, other in peers():
        sums.append(pltpu.make_async_remote_copy(
            src_ref=block, dst_ref=blocks.at[step], send_sem=send_sum.at[step], recv_sem=recv_sum.at[step],
            device_id={"grp": other}, device_id_type=MESH))
        sums[-1].start()
    for c in range(CHUNKS):
        for copy in slabs[c] + [ahead[c], back[c], on[c]] + [k for w in range(2) for k in picks[w][c] + sends[w][c]]:
            copy.wait_send()

        @pl.when(even)
        def _():
            side[c][0].wait_send()

        @pl.when(jnp.logical_not(even))
        def _():
            side[c][1].wait_send()

    for copy in sums:
        copy.wait()
    total_ref[...] = ((block[...] + blocks[2]) + (blocks[1] + blocks[3])) / float(B**3)


def exchange(orbitals, kernel, anchors, count, first, second, reach):
    left, inverse, right, twiddle = (jnp.asarray(t) for t in tables())
    vmem, hbm = pl.BlockSpec(memory_space=pltpu.VMEM), pl.BlockSpec(memory_space=pltpu.HBM)
    dma, f32, bf16 = pltpu.SemaphoreType.DMA, jnp.float32, jnp.bfloat16
    per_chunk, per_peer = dma((CHUNKS,)), dma((CHUNKS, GRP))
    part = pltpu.VMEM((FRAG, CHUNK, 128), f32)
    return pl.pallas_call(
        exchange_kernel,
        out_shape=(jax.ShapeDtypeStruct((FRAG, SLAB, 128), f32),
                   jax.ShapeDtypeStruct((FRAG, SLAB, 128), f32),
                   jax.ShapeDtypeStruct((FRAG, 128), f32)),
        in_specs=[hbm] * 11,
        out_specs=(vmem, vmem, vmem),
        scratch_shapes=[part] * (3 * CHUNKS)
        + [pltpu.VMEM((GRP, TURNS, CHUNK, 128), f32)] * (2 * CHUNKS)
        + [pltpu.VMEM((GRP, TURNS, 2, CHUNK, 128), f32)] * CHUNKS
        + [part] * (4 * CHUNKS)
        + [pltpu.VMEM(a.shape, a.dtype) for a in (orbitals, kernel, left, inverse, right, twiddle)]
        + [pltpu.SMEM(a.shape, a.dtype) for a in (anchors, count, first, second, reach)]
        + [pltpu.VMEM((2, ROWS, 128), f32),
           pltpu.VMEM((TURNS, 2, ROWS, 128), f32),
           pltpu.VMEM((TURNS, 2, ROWS, 128), f32),
           pltpu.VMEM((CH, 384), f32),
           pltpu.VMEM((288, 384), f32),
           pltpu.VMEM((288, 384), f32),
           pltpu.VMEM((2 * CH, 864), bf16),
           pltpu.VMEM((288, 912), bf16),
           pltpu.VMEM((1152, 768), bf16),
           pltpu.VMEM((2, CH, 384), f32),
           pltpu.VMEM((TILES + 2 * PADT, B + 2 * PADX, 128), f32),
           pltpu.VMEM((TURNS, TILES, B, 128), f32),
           pltpu.VMEM((912, 768), bf16),
           pltpu.VMEM((2 * TURNS * CH, 1152), bf16),
           pltpu.VMEM((2 * TURNS * CH, 768), f32),
           pltpu.VMEM((2 * CH, 768), f32),
           pltpu.VMEM((FRAG, FRAG, 8, 128), f32),
           pltpu.VMEM((FRAG, 128), f32),
           pltpu.VMEM((GRP, FRAG, 128), f32),
           dma((11,)), per_peer, per_peer, per_chunk, per_chunk, per_chunk, per_chunk, per_chunk,
           dma((2, CHUNKS, GRP)), dma((2, CHUNKS, GRP)), dma((2, CHUNKS, GRP)), dma((2, CHUNKS, GRP)),
           per_chunk, per_chunk, per_chunk, per_chunk, dma((GRP,)), dma((GRP,))],
        compiler_params=pltpu.CompilerParams(collective_id=0, has_side_effects=True, vmem_limit_bytes=48 << 20),
        name="exchange",
    )(orbitals, kernel, left, inverse, right, twiddle, anchors, count, first, second, reach)


def project_kernel(phi_ref, action_ref, total_ref, gradient_ref, lagrange_ref, flat):
    total = total_ref[...][:, 0:FRAG]
    lagrange = 0.5 * (total + total.T)
    lagrange_ref[0] = lagrange
    for a in range(FRAG):
        value = action_ref[a]
        for b in range(FRAG):
            value = value - lagrange[b:b + 1, a:a + 1] * phi_ref[b]
        flat[SLAB * a:SLAB * a + SLAB, :] = value
    for x in range(12):
        for t in range(TILES):
            gradient_ref[FRAG * x:FRAG * x + FRAG, 128 * t:128 * t + 128] = flat[pl.ds(TILES * x + t, FRAG, stride=SLAB), :]


def projected(phi, action, total):
    vmem = pl.BlockSpec(memory_space=pltpu.VMEM)
    return pl.pallas_call(
        project_kernel,
        out_shape=(jax.ShapeDtypeStruct((12 * FRAG, B * B), jnp.float32),
                   jax.ShapeDtypeStruct((1, FRAG, FRAG), jnp.float32)),
        in_specs=[vmem] * 3,
        out_specs=(vmem, vmem),
        scratch_shapes=[pltpu.VMEM((FRAG * SLAB, 128), jnp.float32)],
        compiler_params=pltpu.CompilerParams(vmem_limit_bytes=8 << 20),
        name="projected",
    )(phi, action, total)


def shards(orbitals, kernel, anchors, pair_count, pair_first, pair_second, pair_reach):
    phi, action, total = exchange(orbitals, kernel, anchors.T, pair_count, pair_first, pair_second, pair_reach)
    gradient, lagrange = projected(phi, action, total)
    return gradient.reshape(12, FRAG, B * B).transpose(1, 0, 2), lagrange


def solution(mesh):
    placed = (P(("orb", "grp"), None, None), P(), P(), P("orb"), P("orb"), P("orb"), P("orb"))
    return jax.shard_map(
        shards,
        mesh=mesh,
        in_specs=placed,
        out_specs=(P("orb", "grp", None), P("orb", None, None)),
        check_vma=False,
    )
```

time: 95.4 us -> 95.3 us (level)
  Pallas kernels: 89.1 us -> 84.8 us
  local copies, waits for them, and re-layouts: 4.71 us -> 8.81 us
    unnamed x24 -> x20, local copies, waits for them, and re-layouts: 3.33 us -> 8.81 us
    pallas_call x4 -> x1, Pallas kernels: 87.2 us -> 82.9 us  [exchange(): pl.pallas_call(exchange_kernel, out_shape=(jax.ShapeDtypeStruct((FRAG, SL...]
    reshape x1 -> x0, local copies, waits for them, and re-layouts: 1.38 us -> none  [shards(): mine = orbitals.reshape(2, GRP, SLAB, 128)]
where the time goes in v4:
time: 95.3 us; the launch traced here: 94.9 us
  Pallas kernels  84.8 us (89%)
  local copies, waits for them, and re-layouts  8.81 us (9%)
  between operations  1.3 us (1%)
    pallas_call x1, Pallas kernels, exchange(): pl.pallas_call(exchange_kernel, out_shape=(jax.ShapeDtypeStruct((FRAG, SL...  82.9 us
    unnamed x20, local copies, waits for them, and re-layouts  8.81 us
    pallas_call x1, Pallas kernels, projected(): pl.pallas_call(project_kernel, out_shape=(jax.ShapeDtypeStruct((12 * FRAG...  1.93 us

profile of v4, /device:TPU:1, one launch (start us, length us, event | category | flops | bytes accessed | tf_op | source)
XLA Modules:
  0.0 94.9 jit_solution(10282850939151182974)
XLA Ops:
  1.3 0.0 copy-start
  1.3 1.3 %copy-done = bf16[768,768]{1,0:T(8,128)(2,1)S(1)} copy-done((bf16[768,768]{1,0:T(8,128)(2,1)S(1)}, bf16[768,768]{1,0:T(8,128)(2,1)}, u32[]{:S(2)}) %copy-start) | copy-done | bytes 1179672
  2.6 0.0 copy-start.1
  2.6 1.2 %copy-done.1 = f32[2,48,2304]{2,1,0:T(8,128)S(1)} copy-done((f32[2,48,2304]{2,1,0:T(8,128)S(1)}, f32[2,48,2304]{2,1,0:T(8,128)}, u32[]{:S(2)}) %copy-start.1) | copy-done | bytes 884760
  3.7 0.0 copy-start.2
  3.7 1.0 %copy-done.2 = f32[48,2304]{1,0:T(8,128)S(1)} copy-done((f32[48,2304]{1,0:T(8,128)S(1)}, f32[48,2304]{1,0:T(8,128)}, u32[]{:S(2)}) %copy-start.2) | copy-done | bytes 442392
  4.7 0.0 copy-start.3
  4.7 1.0 %copy-done.3 = bf16[304,576]{1,0:T(8,128)(2,1)S(1)} copy-done((bf16[304,576]{1,0:T(8,128)(2,1)S(1)}, bf16[304,576]{1,0:T(8,128)(2,1)}, u32[]{:S(2)}) %copy-start.3) | copy-done | bytes 350232
  5.7 0.0 copy-start.4
  5.7 1.0 %copy-done.4 = bf16[288,608]{1,0:T(8,128)(2,1)S(1)} copy-done((bf16[288,608]{1,0:T(8,128)(2,1)S(1)}, bf16[288,608]{1,0:T(8,128)(2,1)}, u32[]{:S(2)}) %copy-start.4) | copy-done | bytes 350232
  6.7 0.0 copy-start.5
  6.7 0.7 copy-done.5
  7.5 0.0 copy-start.6
  7.5 0.7 copy-done.6
  8.1 0.0 copy-start.7
  8.1 0.7 copy-done.7
  8.8 0.0 copy-start.8
  8.8 0.7 copy-done.8
  9.4 0.0 copy-start.9
  9.4 0.7 copy-done.9
  10.1 82.9 %exchange.1 = (f32[8,216,128]{2,1,0:T(8,128)S(1)}, f32[8,216,128]{2,1,0:T(8,128)S(1)}, f32[8,128]{1,0:T(8,128)S(1)}) custom-call(f32[2,48,2304]{2,1,0:T(8,128)S(1)} %copy-done.1, f32[48,2304]{1,0:T(8,128)S(1)} %copy-done.2, bf16[304,576]{1,0:T(8,128)(2,1)S(1)} %copy-done.3, bf16[288,608]{1,0:T(8,128)(2,1)S(1)} %copy-done.4, bf16[768,768]{1,0:T(8,128)(2,1)S(1)} %copy-done, ...), custom_call_target="tpu_custom_call" | custom-call | tf_op jit(solution)/shard_map/exchange/pallas_call | solution.py:417
  93.0 1.9 %projected.1 = (f32[96,2304]{1,0:T(8,128)}, f32[1,8,8]{2,1,0:T(8,128)}) custom-call(f32[8,216,128]{2,1,0:T(8,128)S(1)} %get-tuple-element.7.phi_ref, f32[8,216,128]{2,1,0:T(8,128)S(1)} %get-tuple-element.8.action_ref, f32[8,128]{1,0:T(8,128)S(1)} %get-tuple-element.9.total_ref), custom_call_target="tpu_custom_call" | custom-call | tf_op jit(solution)/shard_map/projected/pallas_call | solution.py:473
Async XLA Ops:
  1.3 1.3 %copy-start = (bf16[768,768]{1,0:T(8,128)(2,1)S(1)}, bf16[768,768]{1,0:T(8,128)(2,1)}, u32[]{:S(2)}) copy-start(bf16[768,768]{1,0:T(8,128)(2,1)} %constant.10.clone.right_hbm) | copy-start | bytes 3538948
  2.6 1.2 %copy-start.1 = (f32[2,48,2304]{2,1,0:T(8,128)S(1)}, f32[2,48,2304]{2,1,0:T(8,128)}, u32[]{:S(2)}) copy-start(f32[2,48,2304]{2,1,0:T(8,128)} %orbitals.1) | copy-start | bytes 2654212
  3.7 1.0 %copy-start.2 = (f32[48,2304]{1,0:T(8,128)S(1)}, f32[48,2304]{1,0:T(8,128)}, u32[]{:S(2)}) copy-start(f32[48,2304]{1,0:T(8,128)} %kernel.1) | copy-start | bytes 1327108
  4.7 1.0 %copy-start.3 = (bf16[304,576]{1,0:T(8,128)(2,1)S(1)}, bf16[304,576]{1,0:T(8,128)(2,1)}, u32[]{:S(2)}) copy-start(bf16[304,576]{1,0:T(8,128)(2,1)} %constant.8.clone.left_hbm) | copy-start | bytes 1050628
  5.7 1.0 %copy-start.4 = (bf16[288,608]{1,0:T(8,128)(2,1)S(1)}, bf16[288,608]{1,0:T(8,128)(2,1)}, u32[]{:S(2)}) copy-start(bf16[288,608]{1,0:T(8,128)(2,1)} %constant.9.clone.inverse_hbm) | copy-start | bytes 1050628
  6.7 0.7 copy-start.5
  7.5 0.7 copy-start.6
  8.1 0.7 copy-start.7
  8.8 0.7 copy-start.8
  9.4 0.7 copy-start.9

commit v5 on v4

--- a/solution.py
+++ b/solution.py
@@ -177,17 +177,23 @@
     volume[0:288, :] = dot(inverse[...], stack[...])
 
 
-def terms_of(turn, pairs, offset, volume, moved, padded, terms):
+def back_terms(turn, pairs, offset, volume, padded, terms):
     for t in range(TILES):
         rows, lanes = block_of(t)
         potential = volume[rows, 384 * turn + lanes.start:384 * turn + lanes.stop]
-        terms[turn, 0, pl.ds(t, B, stride=TILES), :] = potential * moved[turn, t]
         padded[t + PADT, pl.ds(PADX, B), :] = potential * pairs[turn, 0, pl.ds(t, B, stride=TILES), :]
 
     def emit(t, block):
-        terms[turn, 1, pl.ds(t, B, stride=TILES), :] = block
+        terms[1, turn, pl.ds(t, B, stride=TILES), :] = block
 
     shifted(padded, [-d for d in offset], emit)
+
+
+def forward_terms(turn, volume, moved, terms):
+    for t in range(TILES):
+        rows, lanes = block_of(t)
+        potential = volume[rows, 384 * turn + lanes.start:384 * turn + lanes.stop]
+        terms[0, turn, pl.ds(t, B, stride=TILES), :] = potential * moved[turn, t]
 
 
 def sibling(orb):
@@ -195,7 +201,7 @@
 
 
 def exchange_kernel(orbitals, kernel, left_hbm, inverse_hbm, right_hbm, twiddle_hbm, anchors_hbm, count_hbm, first_hbm,
-                    second_hbm, reach_hbm, phi_ref, action_ref, total_ref, *scratch):
+                    second_hbm, reach_hbm, gradient_ref, lagrange_ref, *scratch):
     scratch = list(scratch)
 
     def take(n):
@@ -204,12 +210,13 @@
 
     near = take(3 * CHUNKS)
     out = take(2 * CHUNKS)
-    landed, aside, beside, onward, behind = (take(CHUNKS) for _ in range(5))
+    landed, landed_back, aside, beside, onward, behind = (take(CHUNKS) for _ in range(6))
+    landed = (landed, landed_back)
     native, kernel_ref, left_ref, inverse_ref, right_ref, twiddle_ref = take(6)
-    anchors, count, first, second, reach = take(5)
+    anchors, count, first, second, reach, weights = take(6)
     mine, pairs, terms, modes, picked, mirrored, left, inverse, right, twiddle = take(10)
     padded, moved, stack, wide, spec, volume = take(6)
-    products, block, blocks = take(3)
+    products, block, blocks, phi, action, flat = take(6)
     (load_sem, send_slab, recv_slab, own_sem, send_ahead, recv_ahead, send_side, recv_side, send_pick, recv_pick,
      send_term, recv_term, send_back, recv_back, send_on, recv_on, send_sum, recv_sum) = scratch
     orb, me = lax.axis_index("orb"), lax.axis_index("grp")
@@ -291,7 +298,7 @@
             side[c][1].start()
 
         choose(0, c)
-        phi_ref[:, CHUNK * c:CHUNK * c + CHUNK, :] = near[3 * c][...]
+        phi[:, CHUNK * c:CHUNK * c + CHUNK, :] = near[3 * c][...]
         if c == 0:
             for load in loads[4:]:
                 load.wait()
@@ -300,6 +307,14 @@
             modes_of(kernel_ref, modes, picked, mirrored)
         if c == 2:
             padded[...] = jnp.zeros_like(padded)
+        if c == 3:
+            for slot in range(GRP * TURNS):
+                live = jnp.where(slot < count[0], 1.0, 0.0)
+                for a in range(FRAG):
+                    weights[0, FRAG * slot + a] = jnp.where(first[slot] == a, live, 0.0)
+                    hit = jnp.where(second[slot] == a, live, 0.0)
+                    for far in range(3):
+                        weights[1 + far, FRAG * slot + a] = jnp.where(reach[slot] == far, hit, 0.0)
     for c in range(CHUNKS + 1):
         if c < CHUNKS:
             ahead[c].wait_recv()
@@ -323,61 +338,63 @@
     potentials(pairs, offsets, modes, left, inverse, right, twiddle, padded, moved, stack, wide, spec, volume)
 
     sends = [[[pltpu.make_async_remote_copy(
-        src_ref=terms.at[turn, :, at_slab(other, c)], dst_ref=landed[c].at[me, turn],
-        send_sem=send_term.at[turn, c, step], recv_sem=recv_term.at[turn, c, step],
+        src_ref=terms.at[which, :, at_slab(other, c)], dst_ref=landed[which][c].at[me],
+        send_sem=send_term.at[which, c, step], recv_sem=recv_term.at[which, c, step],
         device_id={"grp": other}, device_id_type=MESH) for step, other in peers()]
-        for c in range(CHUNKS)] for turn in range(TURNS)]
-    early = 2
-    for turn in range(TURNS):
-        terms_of(turn, pairs, offsets[turn], volume, moved, padded, terms)
-        for c in range(CHUNKS):
-            for other_turn in range(TURNS):
-                if turn == (0 if other_turn == 0 and c < early else 1):
-                    for copy in sends[other_turn][c]:
-                        copy.start()
+        for c in range(CHUNKS)] for which in range(2)]
+    for turn in range(TURNS):
+        back_terms(turn, pairs, offsets[turn], volume, padded, terms)
+    for c in range(CHUNKS):
+        for copy in sends[1][c]:
+            copy.start()
+    for turn in range(TURNS):
+        forward_terms(turn, volume, moved, terms)
+    for c in range(CHUNKS):
+        for copy in sends[0][c]:
+            copy.start()
     back = [pltpu.make_async_remote_copy(
         src_ref=aside[c], dst_ref=beside[c], send_sem=send_back.at[c], recv_sem=recv_back.at[c],
         device_id={"orb": sibling(orb)}, device_id_type=MESH) for c in range(CHUNKS)]
     on = [pltpu.make_async_remote_copy(
         src_ref=onward[c], dst_ref=behind[c], send_sem=send_on.at[c], recv_sem=recv_on.at[c],
         device_id={"orb": lax.rem(orb + 2, orbs)}, device_id_type=MESH) for c in range(CHUNKS)]
-    live = [jnp.where(slot < count[0], 1.0, 0.0) for slot in range(GRP * TURNS)]
-
-    def summed(c, a, which, far):
+
+    def summed(c, a, kind):
         value = jnp.zeros((CHUNK, 128), jnp.float32)
         for slot in range(GRP * TURNS):
-            term = landed[c][slot % GRP, slot // GRP, which]
-            if which == 0:
-                weight = jnp.where(first[slot] == a, live[slot], 0.0)
-            else:
-                weight = jnp.where((second[slot] == a) & (reach[slot] == far), live[slot], 0.0)
-            value = value + weight * term
+            term = landed[kind > 0][c][slot % GRP, slot // GRP]
+            value = value + weights[kind, FRAG * slot + a] * term
         return value
 
     for c in range(CHUNKS):
-        landed[c][me] = terms[:, :, at_slab(me, c), :]
-    for c in range(CHUNKS):
-        for turn in range(TURNS):
-            for copy in sends[turn][c]:
-                copy.wait_recv()
+        landed[1][c][me] = terms[1, :, at_slab(me, c), :]
+    for c in range(CHUNKS):
+        for copy in sends[1][c]:
+            copy.wait_recv()
         for a in range(FRAG):
-            aside[c][a] = summed(c, a, 1, 1)
+            aside[c][a] = summed(c, a, 2)
         back[c].start()
         for a in range(FRAG):
-            onward[c][a] = summed(c, a, 1, 2)
-            action_ref[a, CHUNK * c:CHUNK * c + CHUNK, :] = summed(c, a, 0, 0) + summed(c, a, 1, 0)
+            onward[c][a] = summed(c, a, 3)
         back[c].wait_recv()
         for a in range(FRAG):
             onward[c][a] = onward[c][a] + is_even * beside[c][a]
         on[c].start()
+        for a in range(FRAG):
+            action[a, CHUNK * c:CHUNK * c + CHUNK, :] = summed(c, a, 1) + (1.0 - is_even) * beside[c][a]
+        landed[0][c][me] = terms[0, :, at_slab(me, c), :]
     products[...] = jnp.zeros_like(products)
     for c in range(CHUNKS):
+        for copy in sends[0][c]:
+            copy.wait_recv()
+        for b in range(FRAG):
+            action[b, CHUNK * c:CHUNK * c + CHUNK, :] += summed(c, b, 0)
         on[c].wait_recv()
         for b in range(FRAG):
-            value = action_ref[b, CHUNK * c:CHUNK * c + CHUNK, :] + behind[c][b] + (1.0 - is_even) * beside[c][b]
-            action_ref[b, CHUNK * c:CHUNK * c + CHUNK, :] = value
+            value = action[b, CHUNK * c:CHUNK * c + CHUNK, :] + behind[c][b]
+            action[b, CHUNK * c:CHUNK * c + CHUNK, :] = value
             for a in range(FRAG):
-                part = jnp.sum((phi_ref[a, CHUNK * c:CHUNK * c + CHUNK, :] * value).reshape(CHUNK // 8, 8, 128), axis=0)
+                part = jnp.sum((phi[a, CHUNK * c:CHUNK * c + CHUNK, :] * value).reshape(CHUNK // 8, 8, 128), axis=0)
                 products[b, a] = products[b, a] + part
     lane = lax.broadcasted_iota(jnp.int32, (FRAG, 128), 1)
     total = jnp.zeros((FRAG, 128), jnp.float32)
@@ -405,7 +422,17 @@
 
     for copy in sums:
         copy.wait()
-    total_ref[...] = ((block[...] + blocks[2]) + (blocks[1] + blocks[3])) / float(B**3)
+    total = (((block[...] + blocks[2]) + (blocks[1] + blocks[3])) / float(B**3))[:, 0:FRAG]
+    lagrange = 0.5 * (total + total.T)
+    lagrange_ref[0] = lagrange
+    for a in range(FRAG):
+        value = action[a]
+        for b in range(FRAG):
+            value = value - lagrange[b:b + 1, a:a + 1] * phi[b]
+        flat[SLAB * a:SLAB * a + SLAB, :] = value
+    for x in range(12):
+        for t in range(TILES):
+            gradient_ref[FRAG * x:FRAG * x + FRAG, 128 * t:128 * t + 128] = flat[pl.ds(TILES * x + t, FRAG, stride=SLAB), :]
 
 
 def exchange(orbitals, kernel, anchors, count, first, second, reach):
@@ -416,17 +443,16 @@
     part = pltpu.VMEM((FRAG, CHUNK, 128), f32)
     return pl.pallas_call(
         exchange_kernel,
-        out_shape=(jax.ShapeDtypeStruct((FRAG, SLAB, 128), f32),
-                   jax.ShapeDtypeStruct((FRAG, SLAB, 128), f32),
-                   jax.ShapeDtypeStruct((FRAG, 128), f32)),
+        out_shape=(jax.ShapeDtypeStruct((12 * FRAG, B * B), f32), jax.ShapeDtypeStruct((1, FRAG, FRAG), f32)),
         in_specs=[hbm] * 11,
-        out_specs=(vmem, vmem, vmem),
+        out_specs=(vmem, vmem),
         scratch_shapes=[part] * (3 * CHUNKS)
         + [pltpu.VMEM((GRP, TURNS, CHUNK, 128), f32)] * (2 * CHUNKS)
-        + [pltpu.VMEM((GRP, TURNS, 2, CHUNK, 128), f32)] * CHUNKS
+        + [pltpu.VMEM((GRP, TURNS, CHUNK, 128), f32)] * (2 * CHUNKS)
         + [part] * (4 * CHUNKS)
         + [pltpu.VMEM(a.shape, a.dtype) for a in (orbitals, kernel, left, inverse, right, twiddle)]
         + [pltpu.SMEM(a.shape, a.dtype) for a in (anchors, count, first, second, reach)]
+        + [pltpu.SMEM((4, FRAG * GRP * TURNS), f32)]
         + [pltpu.VMEM((2, ROWS, 128), f32),
            pltpu.VMEM((TURNS, 2, ROWS, 128), f32),
            pltpu.VMEM((TURNS, 2, ROWS, 128), f32),
@@ -446,45 +472,19 @@
            pltpu.VMEM((FRAG, FRAG, 8, 128), f32),
            pltpu.VMEM((FRAG, 128), f32),
            pltpu.VMEM((GRP, FRAG, 128), f32),
+           pltpu.VMEM((FRAG, SLAB, 128), f32),
+           pltpu.VMEM((FRAG, SLAB, 128), f32),
+           pltpu.VMEM((FRAG * SLAB, 128), f32),
            dma((11,)), per_peer, per_peer, per_chunk, per_chunk, per_chunk, per_chunk, per_chunk,
            dma((2, CHUNKS, GRP)), dma((2, CHUNKS, GRP)), dma((2, CHUNKS, GRP)), dma((2, CHUNKS, GRP)),
            per_chunk, per_chunk, per_chunk, per_chunk, dma((GRP,)), dma((GRP,))],
-        compiler_params=pltpu.CompilerParams(collective_id=0, has_side_effects=True, vmem_limit_bytes=48 << 20),
+        compiler_params=pltpu.CompilerParams(collective_id=0, has_side_effects=True, vmem_limit_bytes=67043328),
         name="exchange",
     )(orbitals, kernel, left, inverse, right, twiddle, anchors, count, first, second, reach)
 
 
-def project_kernel(phi_ref, action_ref, total_ref, gradient_ref, lagrange_ref, flat):
-    total = total_ref[...][:, 0:FRAG]
-    lagrange = 0.5 * (total + total.T)
-    lagrange_ref[0] = lagrange
-    for a in range(FRAG):
-        value = action_ref[a]
-        for b in range(FRAG):
-            value = value - lagrange[b:b + 1, a:a + 1] * phi_ref[b]
-        flat[SLAB * a:SLAB * a + SLAB, :] = value
-    for x in range(12):
-        for t in range(TILES):
-            gradient_ref[FRAG * x:FRAG * x + FRAG, 128 * t:128 * t + 128] = flat[pl.ds(TILES * x + t, FRAG, stride=SLAB), :]
-
-
-def projected(phi, action, total):
-    vmem = pl.BlockSpec(memory_space=pltpu.VMEM)
-    return pl.pallas_call(
-        project_kernel,
-        out_shape=(jax.ShapeDtypeStruct((12 * FRAG, B * B), jnp.float32),
-                   jax.ShapeDtypeStruct((1, FRAG, FRAG), jnp.float32)),
-        in_specs=[vmem] * 3,
-        out_specs=(vmem, vmem),
-        scratch_shapes=[pltpu.VMEM((FRAG * SLAB, 128), jnp.float32)],
-        compiler_params=pltpu.CompilerParams(vmem_limit_bytes=8 << 20),
-        name="projected",
-    )(phi, action, total)
-
-
 def shards(orbitals, kernel, anchors, pair_count, pair_first, pair_second, pair_reach):
-    phi, action, total = exchange(orbitals, kernel, anchors.T, pair_count, pair_first, pair_second, pair_reach)
-    gradient, lagrange = projected(phi, action, total)
+    gradient, lagrange = exchange(orbitals, kernel, anchors.T, pair_count, pair_first, pair_second, pair_reach)
     return gradient.reshape(12, FRAG, B * B).transpose(1, 0, 2), lagrange
 
 

time: 95.3 us -> 85.9 us (0.901)
  local copies, waits for them, and re-layouts: 8.81 us -> 2.73 us
  Pallas kernels: 84.8 us -> 81.8 us
    unnamed x20 -> x4, local copies, waits for them, and re-layouts: 8.81 us -> 2.73 us
    pallas_call x2 -> x1, Pallas kernels: 84.8 us -> 81.8 us  [exchange(): pl.pallas_call(exchange_kernel, out_shape=(jax.ShapeDtypeStruct((12 * FRA...]
where the time goes in v5:
time: 85.9 us; the launch traced here: 85.8 us
  Pallas kernels  81.8 us (95%)
  local copies, waits for them, and re-layouts  2.73 us (3%)
  between operations  1.29 us (2%)
    pallas_call x1, Pallas kernels, exchange(): pl.pallas_call(exchange_kernel, out_shape=(jax.ShapeDtypeStruct((12 * FRA...  81.8 us
    unnamed x4, local copies, waits for them, and re-layouts  2.73 us

profile of v5, /device:TPU:1, one launch (start us, length us, event | category | flops | bytes accessed | tf_op | source)
XLA Modules:
  0.0 85.8 jit_solution(15651632939423665463)
XLA Ops:
  1.3 81.8 %exchange.1 = (f32[96,2304]{1,0:T(8,128)}, f32[1,8,8]{2,1,0:T(8,128)}) custom-call(f32[2,48,2304]{2,1,0:T(8,128)} %orbitals.1, f32[48,2304]{1,0:T(8,128)} %kernel.1, bf16[304,576]{1,0:T(8,128)(2,1)} %constant.8.clone.left_hbm, bf16[288,608]{1,0:T(8,128)(2,1)} %constant.9.clone.inverse_hbm, bf16[768,768]{1,0:T(8,128)(2,1)} %constant.10.clone.right_hbm, ...), custom_call_target="tpu_custom_call" | custom-call | tf_op jit(solution)/shard_map/exchange/pallas_call | solution.py:444
  83.0 0.0 copy-start
  83.1 2.1 %copy.16 = f32[8,12,2304]{2,0,1:T(8,128)} copy(f32[8,12,2304]{2,0,1:T(8,128)} %bitcast.4) | data formatting | bytes 1769472
  85.2 0.0 copy-done
  85.2 0.6 copy.17
Async XLA Ops:
  83.0 2.1 %copy-start = (f32[1,8,8]{2,1,0:T(8,128)S(1)}, f32[1,8,8]{2,1,0:T(8,128)}, u32[]{:S(2)}) copy-start(f32[1,8,8]{2,1,0:T(8,128)} %get-tuple-element.9) | copy-start | bytes 772

commit v6 on v5

--- a/solution.py
+++ b/solution.py
@@ -22,8 +22,12 @@
 CH = 152
 PADX = 16
 PADT = 8
-CHUNKS = 9
-CHUNK = SLAB // CHUNKS
+BANDS = 3
+AHEAD_Y = 9
+AHEAD_Z = 4
+PARTS = (24, 40, 40, 40, 40, 32)
+CHUNKS = len(PARTS)
+STARTS = tuple(sum(PARTS[:c]) for c in range(CHUNKS))
 
 
 def split(a):
@@ -201,7 +205,7 @@
 
 
 def exchange_kernel(orbitals, kernel, left_hbm, inverse_hbm, right_hbm, twiddle_hbm, anchors_hbm, count_hbm, first_hbm,
-                    second_hbm, reach_hbm, gradient_ref, lagrange_ref, *scratch):
+                    second_hbm, reach_hbm, phi_hbm, action_hbm, total_ref, *scratch):
     scratch = list(scratch)
 
     def take(n):
@@ -216,9 +220,9 @@
     anchors, count, first, second, reach, weights = take(6)
     mine, pairs, terms, modes, picked, mirrored, left, inverse, right, twiddle = take(10)
     padded, moved, stack, wide, spec, volume = take(6)
-    products, block, blocks, phi, action, flat = take(6)
+    products, block, blocks, action, phi_rows, action_rows = take(6)
     (load_sem, send_slab, recv_slab, own_sem, send_ahead, recv_ahead, send_side, recv_side, send_pick, recv_pick,
-     send_term, recv_term, send_back, recv_back, send_on, recv_on, send_sum, recv_sum) = scratch
+     send_term, recv_term, out_sem, send_back, recv_back, send_on, recv_on, send_sum, recv_sum) = scratch
     orb, me = lax.axis_index("orb"), lax.axis_index("grp")
     orbs = lax.axis_size("orb")
     even = lax.rem(orb, 2) == 0
@@ -241,13 +245,13 @@
     pl.semaphore_wait(barrier, GRP - 1 + 3)
 
     def rows(c):
-        return pl.ds(CHUNK * c, CHUNK)
+        return pl.ds(STARTS[c], PARTS[c])
 
     def peers():
         return [(step, lax.rem(me + step, GRP)) for step in (2, 1, 3)]
 
     def at_slab(member, c):
-        return pl.ds(pl.multiple_of(SLAB * member + CHUNK * c, 8), CHUNK)
+        return pl.ds(pl.multiple_of(SLAB * member + STARTS[c], 8), PARTS[c])
 
     slabs, owns = [], []
     for c in range(CHUNKS):
@@ -257,8 +261,9 @@
             device_id={"grp": other}, device_id_type=MESH) for step, other in peers()])
         owns.append(pltpu.make_async_copy(mine.at[:, at_slab(me, c)], near[3 * c].at[pl.ds(2 * me, 2)], own_sem.at[c]))
         owns[c].start()
-        for copy in slabs[c]:
-            copy.start()
+        if c < AHEAD_Y:
+            for copy in slabs[c]:
+                copy.start()
 
     ahead = [pltpu.make_async_remote_copy(
         src_ref=near[3 * c], dst_ref=near[3 * c + 2], send_sem=send_ahead.at[c], recv_sem=recv_ahead.at[c],
@@ -271,6 +276,19 @@
         send_sem=send_pick.at[which, c, step], recv_sem=recv_pick.at[which, c, step],
         device_id={"grp": other}, device_id_type=MESH) for step, other in peers()]
         for c in range(CHUNKS)] for which in range(2)]
+
+    bands = 3
+    band = 12 * FRAG // bands
+    phi_outs, action_outs = ([pltpu.make_async_copy(
+        ref.at[pl.ds(band * k, band)], place.at[pl.ds(band * k, band)], out_sem.at[i, k]) for k in range(bands)]
+        for i, (ref, place) in enumerate(((phi_rows, phi_hbm), (action_rows, action_hbm))))
+
+    def lay(source, c, rows_ref, outs):
+        for r in range(STARTS[c], STARTS[c] + PARTS[c]):
+            x, t = r // TILES, r % TILES
+            rows_ref[FRAG * x:FRAG * x + FRAG, 128 * t:128 * t + 128] = source(r)
+            if (r + 1) % (SLAB // bands) == 0:
+                outs[r // (SLAB // bands)].start()
 
     def choose(which, c):
         for slot in range(GRP * TURNS):
@@ -287,18 +305,23 @@
 
     for load in loads[1:4]:
         load.wait()
-    for c in range(CHUNKS):
-        owns[c].wait()
-        for copy in slabs[c]:
-            copy.wait_recv()
-        ahead[c].start()
-
-        @pl.when(jnp.logical_not(even))
-        def _():
-            side[c][1].start()
-
-        choose(0, c)
-        phi[:, CHUNK * c:CHUNK * c + CHUNK, :] = near[3 * c][...]
+    for tick in range(CHUNKS + AHEAD_Z + 1):
+        c = tick
+        if c < CHUNKS:
+            owns[c].wait()
+            for copy in slabs[c]:
+                copy.wait_recv()
+            ahead[c].start()
+
+            @pl.when(jnp.logical_not(even))
+            def _():
+                side[c][1].start()
+
+            if c + AHEAD_Y < CHUNKS:
+                for copy in slabs[c + AHEAD_Y]:
+                    copy.start()
+            choose(0, c)
+            lay(lambda r: near[3 * c][:, r - STARTS[c], :], c, phi_rows, phi_outs)
         if c == 0:
             for load in loads[4:]:
                 load.wait()
@@ -315,17 +338,18 @@
                     hit = jnp.where(second[slot] == a, live, 0.0)
                     for far in range(3):
                         weights[1 + far, FRAG * slot + a] = jnp.where(reach[slot] == far, hit, 0.0)
-    for c in range(CHUNKS + 1):
-        if c < CHUNKS:
+        c = tick - AHEAD_Z
+        if 0 <= c < CHUNKS:
             ahead[c].wait_recv()
 
             @pl.when(even)
             def _():
                 side[c][0].start()
 
-        if c > 0:
-            side[c - 1][0].wait_recv()
-            choose(1, c - 1)
+        c = tick - AHEAD_Z - 1
+        if 0 <= c < CHUNKS:
+            side[c][0].wait_recv()
+            choose(1, c)
     for c in range(CHUNKS):
         for which in range(2):
             for copy in picks[which][c]:
@@ -344,14 +368,11 @@
         for c in range(CHUNKS)] for which in range(2)]
     for turn in range(TURNS):
         back_terms(turn, pairs, offsets[turn], volume, padded, terms)
-    for c in range(CHUNKS):
+    for c in range(min(AHEAD_Y, CHUNKS)):
         for copy in sends[1][c]:
             copy.start()
     for turn in range(TURNS):
         forward_terms(turn, volume, moved, terms)
-    for c in range(CHUNKS):
-        for copy in sends[0][c]:
-            copy.start()
     back = [pltpu.make_async_remote_copy(
         src_ref=aside[c], dst_ref=beside[c], send_sem=send_back.at[c], recv_sem=recv_back.at[c],
         device_id={"orb": sibling(orb)}, device_id_type=MESH) for c in range(CHUNKS)]
@@ -360,42 +381,50 @@
         device_id={"orb": lax.rem(orb + 2, orbs)}, device_id_type=MESH) for c in range(CHUNKS)]
 
     def summed(c, a, kind):
-        value = jnp.zeros((CHUNK, 128), jnp.float32)
+        value = jnp.zeros((PARTS[c], 128), jnp.float32)
         for slot in range(GRP * TURNS):
             term = landed[kind > 0][c][slot % GRP, slot // GRP]
             value = value + weights[kind, FRAG * slot + a] * term
         return value
 
+    products[...] = jnp.zeros_like(products)
     for c in range(CHUNKS):
         landed[1][c][me] = terms[1, :, at_slab(me, c), :]
-    for c in range(CHUNKS):
-        for copy in sends[1][c]:
-            copy.wait_recv()
-        for a in range(FRAG):
-            aside[c][a] = summed(c, a, 2)
-        back[c].start()
-        for a in range(FRAG):
-            onward[c][a] = summed(c, a, 3)
-        back[c].wait_recv()
-        for a in range(FRAG):
-            onward[c][a] = onward[c][a] + is_even * beside[c][a]
-        on[c].start()
-        for a in range(FRAG):
-            action[a, CHUNK * c:CHUNK * c + CHUNK, :] = summed(c, a, 1) + (1.0 - is_even) * beside[c][a]
-        landed[0][c][me] = terms[0, :, at_slab(me, c), :]
-    products[...] = jnp.zeros_like(products)
-    for c in range(CHUNKS):
-        for copy in sends[0][c]:
-            copy.wait_recv()
-        for b in range(FRAG):
-            action[b, CHUNK * c:CHUNK * c + CHUNK, :] += summed(c, b, 0)
-        on[c].wait_recv()
-        for b in range(FRAG):
-            value = action[b, CHUNK * c:CHUNK * c + CHUNK, :] + behind[c][b]
-            action[b, CHUNK * c:CHUNK * c + CHUNK, :] = value
+    for tick in range(CHUNKS + AHEAD_Z):
+        c = tick
+        if c < CHUNKS:
+            for copy in sends[1][c]:
+                copy.wait_recv()
+            for copy in (sends[1][c + AHEAD_Y] if c + AHEAD_Y < CHUNKS else []):
+                copy.start()
             for a in range(FRAG):
-                part = jnp.sum((phi[a, CHUNK * c:CHUNK * c + CHUNK, :] * value).reshape(CHUNK // 8, 8, 128), axis=0)
-                products[b, a] = products[b, a] + part
+                aside[c][a] = summed(c, a, 2)
+            back[c].start()
+            for a in range(FRAG):
+                onward[c][a] = summed(c, a, 3)
+            back[c].wait_recv()
+            for a in range(FRAG):
+                onward[c][a] = onward[c][a] + is_even * beside[c][a]
+            on[c].start()
+            for copy in sends[0][c]:
+                copy.start()
+            for a in range(FRAG):
+                action[a, STARTS[c]:STARTS[c] + PARTS[c], :] = summed(c, a, 1) + (1.0 - is_even) * beside[c][a]
+            landed[0][c][me] = terms[0, :, at_slab(me, c), :]
+        c = tick - AHEAD_Z
+        if c >= 0:
+            for copy in sends[0][c]:
+                copy.wait_recv()
+            for b in range(FRAG):
+                action[b, STARTS[c]:STARTS[c] + PARTS[c], :] += summed(c, b, 0)
+            on[c].wait_recv()
+            for b in range(FRAG):
+                value = action[b, STARTS[c]:STARTS[c] + PARTS[c], :] + behind[c][b]
+                action[b, STARTS[c]:STARTS[c] + PARTS[c], :] = value
+                for a in range(FRAG):
+                    part = jnp.sum((near[3 * c][a] * value).reshape(PARTS[c] // 8, 8, 128), axis=0)
+                    products[b, a] = products[b, a] + part
+            lay(lambda r: action[:, r, :], c, action_rows, action_outs)
     lane = lax.broadcasted_iota(jnp.int32, (FRAG, 128), 1)
     total = jnp.zeros((FRAG, 128), jnp.float32)
     for b in range(FRAG):
@@ -420,19 +449,9 @@
         def _():
             side[c][1].wait_send()
 
-    for copy in sums:
+    for copy in sums + phi_outs + action_outs:
         copy.wait()
-    total = (((block[...] + blocks[2]) + (blocks[1] + blocks[3])) / float(B**3))[:, 0:FRAG]
-    lagrange = 0.5 * (total + total.T)
-    lagrange_ref[0] = lagrange
-    for a in range(FRAG):
-        value = action[a]
-        for b in range(FRAG):
-            value = value - lagrange[b:b + 1, a:a + 1] * phi[b]
-        flat[SLAB * a:SLAB * a + SLAB, :] = value
-    for x in range(12):
-        for t in range(TILES):
-            gradient_ref[FRAG * x:FRAG * x + FRAG, 128 * t:128 * t + 128] = flat[pl.ds(TILES * x + t, FRAG, stride=SLAB), :]
+    total_ref[...] = ((block[...] + blocks[2]) + (blocks[1] + blocks[3])) / float(B**3)
 
 
 def exchange(orbitals, kernel, anchors, count, first, second, reach):
@@ -440,16 +459,18 @@
     vmem, hbm = pl.BlockSpec(memory_space=pltpu.VMEM), pl.BlockSpec(memory_space=pltpu.HBM)
     dma, f32, bf16 = pltpu.SemaphoreType.DMA, jnp.float32, jnp.bfloat16
     per_chunk, per_peer = dma((CHUNKS,)), dma((CHUNKS, GRP))
-    part = pltpu.VMEM((FRAG, CHUNK, 128), f32)
+    part = [pltpu.VMEM((FRAG, rows, 128), f32) for rows in PARTS]
+    pick = [pltpu.VMEM((GRP, TURNS, rows, 128), f32) for rows in PARTS]
     return pl.pallas_call(
         exchange_kernel,
-        out_shape=(jax.ShapeDtypeStruct((12 * FRAG, B * B), f32), jax.ShapeDtypeStruct((1, FRAG, FRAG), f32)),
+        out_shape=(jax.ShapeDtypeStruct((12 * FRAG, B * B), f32),
+                   jax.ShapeDtypeStruct((12 * FRAG, B * B), f32),
+                   jax.ShapeDtypeStruct((FRAG, 128), f32)),
         in_specs=[hbm] * 11,
-        out_specs=(vmem, vmem),
-        scratch_shapes=[part] * (3 * CHUNKS)
-        + [pltpu.VMEM((GRP, TURNS, CHUNK, 128), f32)] * (2 * CHUNKS)
-        + [pltpu.VMEM((GRP, TURNS, CHUNK, 128), f32)] * (2 * CHUNKS)
-        + [part] * (4 * CHUNKS)
+        out_specs=(hbm, hbm, vmem),
+        scratch_shapes=[p for p in part for _ in range(3)]
+        + [p for p in pick for _ in range(2)]
+        + pick * 2 + part * 4
         + [pltpu.VMEM(a.shape, a.dtype) for a in (orbitals, kernel, left, inverse, right, twiddle)]
         + [pltpu.SMEM(a.shape, a.dtype) for a in (anchors, count, first, second, reach)]
         + [pltpu.SMEM((4, FRAG * GRP * TURNS), f32)]
@@ -473,18 +494,71 @@
            pltpu.VMEM((FRAG, 128), f32),
            pltpu.VMEM((GRP, FRAG, 128), f32),
            pltpu.VMEM((FRAG, SLAB, 128), f32),
-           pltpu.VMEM((FRAG, SLAB, 128), f32),
-           pltpu.VMEM((FRAG * SLAB, 128), f32),
+           pltpu.VMEM((12 * FRAG, B * B), f32),
+           pltpu.VMEM((12 * FRAG, B * B), f32),
            dma((11,)), per_peer, per_peer, per_chunk, per_chunk, per_chunk, per_chunk, per_chunk,
            dma((2, CHUNKS, GRP)), dma((2, CHUNKS, GRP)), dma((2, CHUNKS, GRP)), dma((2, CHUNKS, GRP)),
+           dma((2, CHUNKS)),
            per_chunk, per_chunk, per_chunk, per_chunk, dma((GRP,)), dma((GRP,))],
         compiler_params=pltpu.CompilerParams(collective_id=0, has_side_effects=True, vmem_limit_bytes=67043328),
         name="exchange",
     )(orbitals, kernel, left, inverse, right, twiddle, anchors, count, first, second, reach)
 
 
+def project_kernel(phi_hbm, action_hbm, total_hbm, gradient_hbm, lagrange_hbm, phi, action, gradient, total_ref, lagrange_ref,
+                   load_sem, store_sem, small_sem):
+    band = 12 * FRAG // BANDS
+
+    def at(k):
+        return pl.ds(band * k, band)
+
+    loads = [[pltpu.make_async_copy(s.at[at(k)], d.at[at(k)], load_sem.at[i, k])
+              for i, (s, d) in enumerate(((phi_hbm, phi), (action_hbm, action)))] for k in range(BANDS)]
+    stores = [pltpu.make_async_copy(gradient.at[at(k)], gradient_hbm.at[at(k)], store_sem.at[k]) for k in range(BANDS)]
+    small = pltpu.make_async_copy(total_hbm, total_ref, small_sem.at[0])
+    symmetric = pltpu.make_async_copy(lagrange_ref, lagrange_hbm, small_sem.at[1])
+    small.start()
+    for pair in loads:
+        for load in pair:
+            load.start()
+    small.wait()
+    total = total_ref[...][:, 0:FRAG]
+    lagrange = 0.5 * (total + total.T)
+    lagrange_ref[0] = lagrange
+    symmetric.start()
+    for k in range(BANDS):
+        for load in loads[k]:
+            load.wait()
+        for x in range(band * k // FRAG, band * (k + 1) // FRAG):
+            rows = slice(FRAG * x, FRAG * x + FRAG)
+            value = action[rows, :]
+            for b in range(FRAG):
+                value = value - lagrange[:, b:b + 1] * phi[FRAG * x + b:FRAG * x + b + 1, :]
+            gradient[rows, :] = value
+        stores[k].start()
+    for store in stores + [symmetric]:
+        store.wait()
+
+
+def projected(phi, action, total):
+    hbm, dma = pl.BlockSpec(memory_space=pltpu.HBM), pltpu.SemaphoreType.DMA
+    return pl.pallas_call(
+        project_kernel,
+        out_shape=(jax.ShapeDtypeStruct((12 * FRAG, B * B), jnp.float32),
+                   jax.ShapeDtypeStruct((1, FRAG, FRAG), jnp.float32)),
+        in_specs=[hbm] * 3,
+        out_specs=(hbm, hbm),
+        scratch_shapes=[pltpu.VMEM((12 * FRAG, B * B), jnp.float32)] * 3
+        + [pltpu.VMEM((FRAG, 128), jnp.float32), pltpu.VMEM((1, FRAG, FRAG), jnp.float32),
+           dma((2, BANDS)), dma((BANDS,)), dma((2,))],
+        compiler_params=pltpu.CompilerParams(vmem_limit_bytes=67043328),
+        name="projected",
+    )(phi, action, total)
+
+
 def shards(orbitals, kernel, anchors, pair_count, pair_first, pair_second, pair_reach):
-    gradient, lagrange = exchange(orbitals, kernel, anchors.T, pair_count, pair_first, pair_second, pair_reach)
+    phi, action, total = exchange(orbitals, kernel, anchors.T, pair_count, pair_first, pair_second, pair_reach)
+    gradient, lagrange = projected(phi, action, total)
     return gradient.reshape(12, FRAG, B * B).transpose(1, 0, 2), lagrange
 
 

time: 85.9 us -> 85 us (0.990)
  local copies, waits for them, and re-layouts: 2.73 us -> 0 us
  Pallas kernels: 81.8 us -> 83.6 us
    pallas_call x0 -> x1, Pallas kernels: none -> 2.79 us  [projected(): pl.pallas_call(project_kernel, out_shape=(jax.ShapeDtypeStruct((12 * FRAG...]
    unnamed x4 -> x0, local copies, waits for them, and re-layouts: 2.73 us -> none
    pallas_call x1, Pallas kernels: 81.8 us -> 80.9 us  [exchange(): pl.pallas_call(exchange_kernel, out_shape=(jax.ShapeDtypeStruct((12 * FRA...]
where the time goes in v6:
time: 85 us; the launch traced here: 84.9 us
  Pallas kernels  83.6 us (98%)
  between operations  1.28 us (2%)
    pallas_call x1, Pallas kernels, exchange(): pl.pallas_call(exchange_kernel, out_shape=(jax.ShapeDtypeStruct((12 * FRA...  80.9 us
    pallas_call x1, Pallas kernels, projected(): pl.pallas_call(project_kernel, out_shape=(jax.ShapeDtypeStruct((12 * FRAG...  2.79 us

profile of v6, /device:TPU:1, one launch (start us, length us, event | category | flops | bytes accessed | tf_op | source)
XLA Modules:
  0.0 84.9 jit_solution(5585785604838354756)
XLA Ops:
  1.3 80.9 %exchange.1 = (f32[96,2304]{1,0:T(8,128)}, f32[96,2304]{1,0:T(8,128)}, f32[8,128]{1,0:T(8,128)}) custom-call(f32[2,48,2304]{2,1,0:T(8,128)} %orbitals.1, f32[48,2304]{1,0:T(8,128)} %kernel.1, bf16[304,576]{1,0:T(8,128)(2,1)} %constant.8.clone.left_hbm, bf16[288,608]{1,0:T(8,128)(2,1)} %constant.9.clone.inverse_hbm, ...), custom_call_target="tpu_custom_call" | custom-call | tf_op jit(solution)/shard_map/exchange/pallas_call | solution.py:464
  82.1 2.8 %projected.1 = (f32[96,2304]{1,0:T(8,128)}, f32[1,8,8]{2,1,0:T(8,128)}) custom-call(f32[96,2304]{1,0:T(8,128)} %get-tuple-element.7.phi_hbm, f32[96,2304]{1,0:T(8,128)} %get-tuple-element.8.action_hbm, f32[8,128]{1,0:T(8,128)} %get-tuple-element.9.total_hbm), custom_call_target="tpu_custom_call" | custom-call | tf_op jit(solution)/shard_map/projected/pallas_call | solution.py:545
